TPU v7x, 32 devices: a whole 2x2x4 slice. The times are simulated.
32 devices in a mesh: rows: 8 (over z, y), band: 4 (over x, core).
Axes of the slice: x: 2, y: 2, z: 4, core: 2. Of those that a mesh axis runs over, the one named last changes fastest.
Arguments:
- coupling: bfloat16 [16384, 2560], P('rows', 'band'), may hold values from -1 to 2
- sketch: bfloat16 [16384, 256], P('rows'), may hold values from -256 to 256
Outputs:
- basis_out: bfloat16 [16384, 256], P(('rows', 'band'))
- factor: float32 [256, 256], replicated
All inputs are finite; a program needn't handle non-finite values.
Results may differ from a plain program's by a relative error of at most 0.015.
Values may be sent and summed in bfloat16 or wider, within the bound.
No kernel may reach another device: no remote copies, remote signals or barrier semaphores. Data moves between devices by JAX's collectives and lax.ppermute only.
A program may use at most 256 MiB of HBM per device.

v0:
```python
import functools
import math

import jax
import jax.numpy as jnp
from jax import lax
from jax.experimental import pallas as pl
from jax.experimental.pallas import tpu as pltpu
from jax.sharding import PartitionSpec as P


HB = 1024
TB = 512
HIGHEST = lax.Precision.HIGHEST
F32 = jnp.float32
BF16 = jnp.bfloat16
NB = 64
PIV = 8
VMEM = pl.BlockSpec(memory_space=pltpu.VMEM)
IN_HBM = pl.BlockSpec(memory_space=pltpu.HBM)


def flip(array, axis, bit):
    count = lax.axis_size(axis)
    return lax.ppermute(array, axis, [(i, i ^ bit) for i in range(count)])


def place():
    band = lax.axis_index("band")
    return band, band // 2, band % 2


def tile_rows(base, tile):
    return pl.ds(pl.multiple_of(base + tile * TB, TB), TB)


def run_tiles(base, coupling, field, keep_ref, send_ref):
    band, half, core = place()
    width = coupling.shape[1]
    for tile, out in ((1 - core, send_ref), (core, keep_ref)):
        first = pl.multiple_of(tile * TB + band * width - half * HB, 128)
        out[...] = jnp.dot(
            coupling[tile_rows(base, tile), :],
            field[pl.ds(first, width), :],
            preferred_element_type=F32,
        ).astype(BF16)


def first_kernel(coupling, slab, keep_ref, send_ref, edge_ref, coupling_ref, slab_ref, sems):
    _, half, core = place()
    base = pl.multiple_of((1 - half) * HB, HB)
    late = pl.multiple_of(half * HB, HB)
    loads = [pltpu.make_async_copy(slab, slab_ref, sems.at[0])]
    for slot, start in ((1, base), (2, late)):
        rows = pl.ds(start, HB)
        loads.append(
            pltpu.make_async_copy(coupling.at[rows, :], coupling_ref.at[rows, :], sems.at[slot])
        )
    for load in loads:
        load.start()
    loads[0].wait()
    edge_ref[...] = slab_ref[tile_rows(base, core), :]
    loads[1].wait()
    run_tiles(base, coupling_ref, slab_ref, keep_ref, send_ref)
    loads[2].wait()


def early_kernel(coupling, own, own2, far, far2, keep_ref, send_ref, field):
    _, half, core = place()
    for ref, tile in (
        (own, 2 * half + core),
        (own2, 2 * half + 1 - core),
        (far, 2 * (1 - half) + core),
        (far2, 2 * (1 - half) + 1 - core),
    ):
        field[tile_rows(0, tile), :] = ref[...]
    run_tiles((1 - half) * HB, coupling, field, keep_ref, send_ref)


def late_kernel(coupling, near0, near1, halo, halo2, keep_ref, send_ref, field):
    _, half, core = place()
    near_at, halo_at = (1 - half) * HB, half * HB
    for ref, start, tile in (
        (near0, near_at, core),
        (near1, near_at, 1 - core),
        (halo, halo_at, core),
        (halo2, halo_at, 1 - core),
    ):
        field[tile_rows(start, tile), :] = ref[...]
    run_tiles(half * HB, coupling, field, keep_ref, send_ref)


def late_kernel_slab(coupling, slab, halo, halo2, keep_ref, send_ref, field):
    _, half, core = place()
    near_at, halo_at = pl.multiple_of((1 - half) * HB, HB), half * HB
    field[pl.ds(near_at, HB), :] = slab[pl.ds(pl.multiple_of(half * HB, HB), HB), :]
    for ref, tile in ((halo, core), (halo2, 1 - core)):
        field[tile_rows(halo_at, tile), :] = ref[...]
    run_tiles(half * HB, coupling, field, keep_ref, send_ref)


def product(kernel, coupling, *fields):
    width, columns = coupling.shape[1], fields[0].shape[1]
    first = kernel is first_kernel
    outputs = [jax.ShapeDtypeStruct((TB, columns), BF16)] * 2
    scratch = [pltpu.VMEM((2 * HB, columns), BF16)]
    if first:
        outputs += [outputs[0]] + [
            jax.ShapeDtypeStruct(array.shape, BF16) for array in (coupling, fields[0])
        ]
        scratch = [pltpu.SemaphoreType.DMA((3,))]
    operands = (coupling, *fields)
    if first:
        operands = [pltpu.with_memory_space_constraint(array, pltpu.HBM) for array in operands]
    return pl.pallas_call(
        kernel,
        out_shape=outputs,
        in_specs=[IN_HBM] * 2 if first else [VMEM] * (1 + len(fields)),
        out_specs=[VMEM] * len(outputs),
        scratch_shapes=scratch,
        compiler_params=pltpu.CompilerParams(vmem_limit_bytes=8 << 20),
        cost_estimate=pl.CostEstimate(
            flops=4 * TB * width * columns, bytes_accessed=4 * TB * width, transcendentals=0
        ),
    )(*operands)


def gram_kernel(keep, near, far, second_ref, mine_ref, other_ref, packed):
    core = lax.axis_index("band") % 2
    second = keep[...].astype(F32) + near[...].astype(F32) + far[...].astype(F32)
    second_ref[...] = second
    size = second.shape[1]
    mid = size // 2
    over_rows = (((0,), (0,)), ((), ()))
    top = lax.dot_general(
        second[:, :mid], second, over_rows, precision=HIGHEST, preferred_element_type=F32
    )
    low = lax.dot_general(
        second[:, mid:], second[:, mid:], over_rows, precision=HIGHEST, preferred_element_type=F32
    )
    row = lax.broadcasted_iota(jnp.int32, (mid, mid), 0)
    column = lax.broadcasted_iota(jnp.int32, (mid, mid), 1)
    packed[0:mid, :] = top[:, mid:]
    packed[mid:size, :] = jnp.where(column >= row, top[:, :mid], low)
    diagonal = jnp.sum(jnp.where(column == row, low, 0.0), axis=0, keepdims=True)
    packed[size:, :] = jnp.broadcast_to(diagonal, (16, mid))
    part = mid + 8
    mine_ref[...] = packed[pl.ds(pl.multiple_of(core * part, 8), part), :]
    other_ref[...] = packed[pl.ds(pl.multiple_of((1 - core) * part, 8), part), :]


def gram(keep, near, far):
    rows, size = keep.shape
    part = jax.ShapeDtypeStruct((size // 2 + 8, size // 2), F32)
    return pl.pallas_call(
        gram_kernel,
        out_shape=(jax.ShapeDtypeStruct((rows, size), F32), part, part),
        in_specs=[VMEM] * 3,
        out_specs=(VMEM,) * 3,
        scratch_shapes=[pltpu.VMEM((size + 16, size // 2), F32)],
        name="gram_kernel",
        compiler_params=pltpu.CompilerParams(vmem_limit_bytes=12 << 20),
    )(keep, near, far)


def factor_block(block):
    size = block.shape[0]
    groups = size // 8
    rows = [block[8 * i : 8 * i + 8, :] for i in range(groups)]
    shape = rows[0].shape
    sub = lax.broadcasted_iota(jnp.int32, shape, 0)
    for first in range(0, size, PIV):
        own, at = first // 8, first % 8
        pivots = range(PIV)
        row = [jnp.broadcast_to(rows[own][at + p : at + p + 1, :], shape) for p in pivots]
        column = [
            {
                q: jnp.broadcast_to(rows[q][:, first + p : first + p + 1], shape)
                for q in range(own, groups)
            }
            for p in pivots
        ]
        entry = {
            (p, t): jnp.broadcast_to(column[p][own][at + t : at + t + 1, :], shape)
            for p in pivots
            for t in range(p, PIV)
        }
        upper, scale = {}, []
        for p in pivots:
            scale.append(lax.rsqrt(entry[p, p]))
            for t in range(p + 1, PIV):
                upper[p, t] = entry[p, t] * scale[p]
            for t in range(p + 1, PIV):
                for w in range(t, PIV):
                    entry[t, w] = entry[t, w] - upper[p, t] * upper[p, w]

        def solve(values):
            values = list(values)
            for p in pivots:
                values[p] = values[p] * scale[p]
                for t in range(p + 1, PIV):
                    values[t] = values[t] - upper[p, t] * values[p]
            return values

        done = solve(row)
        for q in range(own, groups):
            new = rows[q]
            if PIV < 8 or q > own:
                weight = solve([column[p][q] for p in pivots])
                total = weight[0] * done[0]
                for p in range(1, PIV):
                    total = total + weight[p] * done[p]
                new = new - total
            if q == own:
                new = jnp.where(sub >= at + PIV, new, rows[q])
                for p in pivots:
                    new = jnp.where(sub == at + p, done[p], new)
            rows[q] = new
    return jnp.concatenate(rows, 0)


def factor_kernel(scale_root, mine, other, second, basis_ref, factor_ref, a_ref, b_ref, packed):
    core = lax.axis_index("band") % 2
    part, mid = mine.shape
    size = 2 * mid
    packed[pl.ds(pl.multiple_of(core * part, 8), part), :] = mine[...]
    packed[pl.ds(pl.multiple_of((1 - core) * part, 8), part), :] = other[...]
    folded = packed[mid:size, :]
    turned = folded.T
    row = lax.broadcasted_iota(jnp.int32, (mid, mid), 0)
    column = lax.broadcasted_iota(jnp.int32, (mid, mid), 1)
    a_ref[0:mid, 0:mid] = jnp.where(column >= row, folded, turned)
    a_ref[0:mid, mid:size] = packed[0:mid, :]
    diagonal = jnp.broadcast_to(packed[size : size + 1, :], (mid, mid))
    a_ref[mid:size, mid:size] = jnp.where(
        column < row, folded, jnp.where(column > row, turned, diagonal)
    )
    a_ref[mid:size, 0:mid] = jnp.zeros((mid, mid), F32)
    row_id = lax.broadcasted_iota(jnp.int32, (size, size), 0)
    col_id = lax.broadcasted_iota(jnp.int32, (size, size), 1)
    b_ref[...] = jnp.where(row_id == col_id, 1.0, 0.0).astype(F32)
    factor_ref[...] = jnp.zeros_like(factor_ref)
    lane = lax.broadcasted_iota(jnp.int32, (NB, 128), 1)
    row = lax.broadcasted_iota(jnp.int32, (NB, 128), 0)
    over_rows = (((0,), (0,)), ((), ()))
    for first in range(0, size, NB):
        after = first + NB
        low = (first // 128) * 128
        shift = first - low
        block = a_ref[first:after, low : low + 128]
        if shift:
            block = pltpu.roll(block, 128 - shift, 1)
        block = jnp.where(lane < NB, block, jnp.where(lane - NB == row, 1.0, 0.0))
        block = factor_block(block)
        diagonal = jnp.where((lane < NB) & (lane >= row), block, 0.0)
        if shift:
            diagonal = pltpu.roll(diagonal, shift, 1)
        solve = jnp.where(lane <= row, pltpu.roll(block, 128 - NB, 1), 0.0)[:, :NB]
        high = low + 128
        right = jnp.dot(
            solve, a_ref[first:after, low:size], precision=HIGHEST, preferred_element_type=F32
        )
        column = lax.broadcasted_iota(jnp.int32, right.shape, 1) + low
        right = jnp.where(column >= after, right, 0.0)
        left = jnp.dot(
            solve, b_ref[first:after, 0:high], precision=HIGHEST, preferred_element_type=F32
        )
        if size > high:
            diagonal = jnp.concatenate([diagonal, jnp.zeros((NB, size - high), F32)], 1)
        factor_ref[first:after, low:size] = (right + diagonal) * (1.0 / scale_root)
        b_ref[first:after, 0:high] = left
        if after < size:
            edge = (after // 128) * 128
            ahead = right[:, edge - low :]
            on_a = lax.dot_general(
                ahead, ahead, over_rows, precision=HIGHEST, preferred_element_type=F32
            )
            on_b = lax.dot_general(
                ahead, left, over_rows, precision=HIGHEST, preferred_element_type=F32
            )
            skip = after - edge
            a_ref[after:size, edge:size] -= on_a[skip:, :]
            b_ref[after:size, 0:high] -= on_b[skip:, :]
    basis = lax.dot_general(
        second[...],
        b_ref[...],
        (((1,), (1,)), ((), ())),
        precision=HIGHEST,
        preferred_element_type=F32,
    )
    basis_ref[...] = (basis * scale_root).astype(BF16)


def factor_and_basis(mine, other, second, scale_root):
    rows, size = second.shape
    return pl.pallas_call(
        functools.partial(factor_kernel, scale_root),
        out_shape=(
            jax.ShapeDtypeStruct((rows, size), BF16),
            jax.ShapeDtypeStruct((size, size), F32),
        ),
        in_specs=[VMEM] * 3,
        out_specs=(VMEM, VMEM),
        scratch_shapes=[
            pltpu.VMEM((size, size), F32),
            pltpu.VMEM((size, size), F32),
            pltpu.VMEM((size + 16, size // 2), F32),
        ],
        name="factor_kernel",
        compiler_params=pltpu.CompilerParams(vmem_limit_bytes=16 << 20),
    )(mine, other, second)


def halo_step(send, swapped):
    slabs, bands = lax.axis_size("rows"), lax.axis_size("band")
    pairs = []
    for r in range(slabs):
        for b in range(bands):
            source = r - 1 if b < bands // 2 else r + 1
            if 0 <= source < slabs:
                pairs.append((source * bands + (b ^ 2 if swapped else b), r * bands + b))
    return lax.ppermute(send, ("rows", "band"), pairs)


def inner_step(halo):
    return flip(halo, "band", 1)


def add16(*parts):
    total = parts[0].astype(F32)
    for part in parts[1:]:
        total = total + part.astype(F32)
    return total.astype(BF16)


def per_device(coupling, sketch):
    slabs = lax.axis_size("rows")
    scale_root = math.sqrt(sketch.shape[0] * slabs)

    keep, send, edge, coupling, sketch = product(first_kernel, coupling, sketch)
    near = flip(send, "band", 1)
    halo = halo_step(edge, False)
    far = flip(add16(keep, near), "band", 2)
    halo2 = inner_step(halo)
    keep, send = product(late_kernel_slab, coupling, sketch, halo, halo2)
    own = add16(keep, flip(send, "band", 1), far)

    across = flip(own, "band", 2)
    halo = halo_step(across, False)
    own2 = flip(own, "band", 1)
    across2 = flip(across, "band", 1)
    keep, send = product(early_kernel, coupling, own, own2, across, across2)
    near = flip(send, "band", 1)
    far = flip(add16(keep, near), "band", 2)
    halo2 = inner_step(halo)
    keep, send = product(late_kernel, coupling, own, own2, halo, halo2)
    near = flip(send, "band", 1)

    second, mine, other = gram(keep, near, far)
    mine = mine + flip(other, "band", 1)
    mine = mine + flip(mine, "band", 2)
    bit = 1
    while bit < slabs:
        mine = mine + flip(mine, "rows", bit)
        bit *= 2
    other = flip(mine, "band", 1)
    return factor_and_basis(mine, other, second, scale_root)


def solution(mesh):
    in_specs = (P("rows", "band"), P("rows", None))
    out_specs = (P(("rows", "band"), None), P())

    return jax.shard_map(
        per_device, mesh=mesh, in_specs=in_specs, out_specs=out_specs, check_vma=False
    )
```

profile of v0, /device:TPU:0, one launch (start us, length us, event | category | flops | bytes accessed | tf_op | source)
XLA Modules:
  0.0 87.2 jit_solution(11245321856950884526)
XLA Ops:
  0.6 2.2 %shard_map.41 = (bf16[512,256]{1,0:T(8,128)(2,1)S(1)}, bf16[512,256]{1,0:T(8,128)(2,1)S(1)}, bf16[512,256]{1,0:T(8,128)(2,1)S(1)}, bf16[2048,640]{1,0:T(8,128)(2,1)S(1)}, bf16[2048,256]{1,0:T(8,128)(2,1)S(1)}) custom-call(bf16[2048,640]{1,0:T(8,128)(2,1)} %coupling.1, bf16[2048,256]{1,0:T(8,128)(2,1)} %slab.1), custom_call_target="tpu_custom_call" | custom-call | flops 335544320 | bytes 1310720 | tf_op jit(solution)/shard_map/pallas_call | solution.py:115
  2.9 4.9 %collective-permute-start = (bf16[512,256]{1,0:T(8,128)(2,1)S(1)}, bf16[512,256]{1,0:T(8,128)(2,1)S(1)}, u32[]{:S(2)}, u32[]{:S(2)}) collective-permute-start(bf16[512,256]{1,0:T(8,128)(2,1)S(1)} %get-tuple-element.18), channel_id=1, source_target_pairs={{6,2},{7,3},{0,4},{1,5},{10,6},{11,7},{4,8},{5,9},{14,10},{15,11},... | collective-permute-start | bytes 786440 | tf_op jit(solution)/shard_map/ppermute | solution.py:322
  7.9 5.5 %collective-permute-done.halo = bf16[512,256]{1,0:T(8,128)(2,1)S(1)} collective-permute-done((bf16[512,256]{1,0:T(8,128)(2,1)S(1)}, bf16[512,256]{1,0:T(8,128)(2,1)S(1)}, u32[]{:S(2)}, u32[]{:S(2)}) %collective-permute-start) | collective-permute-done | bytes 262176 | tf_op jit(solution)/shard_map/ppermute | solution.py:322
  13.4 2.5 %collective-permute-start.4 = (bf16[512,256]{1,0:T(8,128)(2,1)S(1)}, bf16[512,256]{1,0:T(8,128)(2,1)S(1)}, u32[]{:S(2)}, u32[]{:S(2)}) collective-permute-start(bf16[512,256]{1,0:T(8,128)(2,1)S(1)} %add_convert_fusion.2), channel_id=1, source_target_pairs={{0,2},{1,3},{2,0},{3,1},{4,6},{5,7},{6,4},{7,5},{8,10},{9,11},{10,... | collective-permute-start | bytes 786440 | tf_op jit(solution)/shard_map/ppermute | solution.py:25
  15.9 0.7 shard_map.42
  16.6 0.3 collective-permute-start.2
  16.9 6.0 %collective-permute-done.4 = bf16[512,256]{1,0:T(8,128)(2,1)S(1)} collective-permute-done((bf16[512,256]{1,0:T(8,128)(2,1)S(1)}, bf16[512,256]{1,0:T(8,128)(2,1)S(1)}, u32[]{:S(2)}, u32[]{:S(2)}) %collective-permute-start.4) | collective-permute-done | bytes 262176 | tf_op jit(solution)/shard_map/ppermute | solution.py:25
  22.9 0.1 add_convert_fusion.1.near0.own
  23.0 1.8 %collective-permute-start.6 = (bf16[512,256]{1,0:T(8,128)(2,1)S(1)}, bf16[512,256]{1,0:T(8,128)(2,1)S(1)}, u32[]{:S(2)}, u32[]{:S(2)}) collective-permute-start(bf16[512,256]{1,0:T(8,128)(2,1)S(1)} %add_convert_fusion.1.near0.own), channel_id=1, source_target_pairs={{0,2},{1,3},{2,0},{3,1},{4,6},{5,7},{6,4},{7,5},{8,10},{9,11},{10,... | collective-permute-start | bytes 786440 | tf_op jit(solution)/shard_map/ppermute | solution.py:25
  24.8 6.4 %collective-permute-done.6.far = bf16[512,256]{1,0:T(8,128)(2,1)S(1)} collective-permute-done((bf16[512,256]{1,0:T(8,128)(2,1)S(1)}, bf16[512,256]{1,0:T(8,128)(2,1)S(1)}, u32[]{:S(2)}, u32[]{:S(2)}) %collective-permute-start.6) | collective-permute-done | bytes 262176 | tf_op jit(solution)/shard_map/ppermute | solution.py:25
  31.2 4.3 %collective-permute-start.7 = (bf16[512,256]{1,0:T(8,128)(2,1)S(1)}, bf16[512,256]{1,0:T(8,128)(2,1)S(1)}, u32[]{:S(2)}, u32[]{:S(2)}) collective-permute-start(bf16[512,256]{1,0:T(8,128)(2,1)S(1)} %collective-permute-done.6.far), channel_id=1, source_target_pairs={{6,2},{7,3},{0,4},{1,5},{10,6},{11,7},{4,8},{5,9},{14,10},{15,11},... | collective-permute-start | bytes 786440 | tf_op jit(solution)/shard_map/ppermute | solution.py:322
  35.6 0.5 collective-permute-start.10
  36.1 4.2 %collective-permute-done.7.halo = bf16[512,256]{1,0:T(8,128)(2,1)S(1)} collective-permute-done((bf16[512,256]{1,0:T(8,128)(2,1)S(1)}, bf16[512,256]{1,0:T(8,128)(2,1)S(1)}, u32[]{:S(2)}, u32[]{:S(2)}) %collective-permute-start.7) | collective-permute-done | bytes 262176 | tf_op jit(solution)/shard_map/ppermute | solution.py:322
  40.3 0.7 shard_map.44
  41.0 0.6 collective-permute-start.11
  41.6 0.3 collective-permute-done.8.halo2
  41.9 0.7 shard_map.43
  42.5 0.2 collective-permute-start.9
  42.8 2.0 %collective-permute-start.12 = (bf16[512,256]{1,0:T(8,128)(2,1)S(1)}, bf16[512,256]{1,0:T(8,128)(2,1)S(1)}, u32[]{:S(2)}, u32[]{:S(2)}) collective-permute-start(bf16[512,256]{1,0:T(8,128)(2,1)S(1)} %add_convert_fusion), channel_id=1, source_target_pairs={{0,2},{1,3},{2,0},{3,1},{4,6},{5,7},{6,4},{7,5},{8,10},{9,11},{10,... | collective-permute-start | bytes 786440 | tf_op jit(solution)/shard_map/ppermute | solution.py:25
  44.8 6.8 %collective-permute-done.12.far = bf16[512,256]{1,0:T(8,128)(2,1)S(1)} collective-permute-done((bf16[512,256]{1,0:T(8,128)(2,1)S(1)}, bf16[512,256]{1,0:T(8,128)(2,1)S(1)}, u32[]{:S(2)}, u32[]{:S(2)}) %collective-permute-start.12) | collective-permute-done | bytes 262176 | tf_op jit(solution)/shard_map/ppermute | solution.py:25
  51.6 0.7 gram_kernel.1
  52.4 1.2 %collective-permute-done.13 = f32[136,128]{1,0:T(8,128)S(1)} collective-permute-done((f32[136,128]{1,0:T(8,128)S(1)}, f32[136,128]{1,0:T(8,128)S(1)}, u32[]{:S(2)}, u32[]{:S(2)}) %collective-permute-start.13) | collective-permute-done | bytes 69664 | tf_op jit(solution)/shard_map/ppermute | solution.py:25
  53.7 1.8 %collective-permute-start.14 = (f32[136,128]{1,0:T(8,128)S(1)}, f32[136,128]{1,0:T(8,128)S(1)}, u32[]{:S(2)}, u32[]{:S(2)}) collective-permute-start(f32[136,128]{1,0:T(8,128)S(1)} %add.31), channel_id=1, source_target_pairs={{0,2},{1,3},{2,0},{3,1},{4,6},{5,7},{6,4},{7,5},{8,10},{9,11},{10,... | collective-permute-start | bytes 208904 | tf_op jit(solution)/shard_map/ppermute | solution.py:25
  55.5 2.6 %collective-permute-done.14 = f32[136,128]{1,0:T(8,128)S(1)} collective-permute-done((f32[136,128]{1,0:T(8,128)S(1)}, f32[136,128]{1,0:T(8,128)S(1)}, u32[]{:S(2)}, u32[]{:S(2)}) %collective-permute-start.14) | collective-permute-done | bytes 69664 | tf_op jit(solution)/shard_map/ppermute | solution.py:25
  58.1 2.7 %collective-permute-start.15 = (f32[136,128]{1,0:T(8,128)S(1)}, f32[136,128]{1,0:T(8,128)S(1)}, u32[]{:S(2)}, u32[]{:S(2)}) collective-permute-start(f32[136,128]{1,0:T(8,128)S(1)} %add.32), channel_id=1, source_target_pairs={{0,4},{4,0},{8,12},{12,8},{16,20},{20,16},{24,28},{28,24},{1,5},{5... | collective-permute-start | bytes 208904 | tf_op jit(solution)/shard_map/ppermute | solution.py:25
  60.8 2.3 %collective-permute-done.15 = f32[136,128]{1,0:T(8,128)S(1)} collective-permute-done((f32[136,128]{1,0:T(8,128)S(1)}, f32[136,128]{1,0:T(8,128)S(1)}, u32[]{:S(2)}, u32[]{:S(2)}) %collective-permute-start.15) | collective-permute-done | bytes 69664 | tf_op jit(solution)/shard_map/ppermute | solution.py:25
  63.1 2.4 %collective-permute-start.16 = (f32[136,128]{1,0:T(8,128)S(1)}, f32[136,128]{1,0:T(8,128)S(1)}, u32[]{:S(2)}, u32[]{:S(2)}) collective-permute-start(f32[136,128]{1,0:T(8,128)S(1)} %add.33), channel_id=1, source_target_pairs={{0,8},{4,12},{8,0},{12,4},{16,24},{20,28},{24,16},{28,20},{1,9},{5... | collective-permute-start | bytes 208904 | tf_op jit(solution)/shard_map/ppermute | solution.py:25
  65.5 2.3 %collective-permute-done.16 = f32[136,128]{1,0:T(8,128)S(1)} collective-permute-done((f32[136,128]{1,0:T(8,128)S(1)}, f32[136,128]{1,0:T(8,128)S(1)}, u32[]{:S(2)}, u32[]{:S(2)}) %collective-permute-start.16) | collective-permute-done | bytes 69664 | tf_op jit(solution)/shard_map/ppermute | solution.py:25
  67.8 3.8 %collective-permute-start.17 = (f32[136,128]{1,0:T(8,128)S(1)}, f32[136,128]{1,0:T(8,128)S(1)}, u32[]{:S(2)}, u32[]{:S(2)}) collective-permute-start(f32[136,128]{1,0:T(8,128)S(1)} %add.34), channel_id=1, source_target_pairs={{0,16},{4,20},{8,24},{12,28},{16,0},{20,4},{24,8},{28,12},{1,17},{... | collective-permute-start | bytes 208904 | tf_op jit(solution)/shard_map/ppermute | solution.py:25
  71.6 3.0 %collective-permute-done.17 = f32[136,128]{1,0:T(8,128)S(1)} collective-permute-done((f32[136,128]{1,0:T(8,128)S(1)}, f32[136,128]{1,0:T(8,128)S(1)}, u32[]{:S(2)}, u32[]{:S(2)}) %collective-permute-start.17) | collective-permute-done | bytes 69664 | tf_op jit(solution)/shard_map/ppermute | solution.py:25
  74.7 1.2 %collective-permute-done.18.other = f32[136,128]{1,0:T(8,128)S(1)} collective-permute-done((f32[136,128]{1,0:T(8,128)S(1)}, f32[136,128]{1,0:T(8,128)S(1)}, u32[]{:S(2)}, u32[]{:S(2)}) %collective-permute-start.18) | collective-permute-done | bytes 69664 | tf_op jit(solution)/shard_map/ppermute | solution.py:25
  76.0 11.2 %factor_kernel.1 = (bf16[512,256]{1,0:T(8,128)(2,1)}, f32[256,256]{1,0:T(8,128)}) custom-call(f32[136,128]{1,0:T(8,128)S(1)} %add.35.mine, f32[136,128]{1,0:T(8,128)S(1)} %collective-permute-done.18.other, f32[512,256]{1,0:T(8,128)S(1)} %get-tuple-element.29.second), custom_call_target="tpu_custom_call" | custom-call | tf_op jit(solution)/shard_map/factor_kernel/pallas_call | solution.py:296
  (20 shorter events, 0.5 us)
Async XLA Ops:
  2.9 10.5 %collective-permute-start = (bf16[512,256]{1,0:T(8,128)(2,1)S(1)}, bf16[512,256]{1,0:T(8,128)(2,1)S(1)}, u32[]{:S(2)}, u32[]{:S(2)}) collective-permute-start(bf16[512,256]{1,0:T(8,128)(2,1)S(1)} %get-tuple-element.18), channel_id=1, source_target_pairs={{6,2},{7,3},{0,4},{1,5},{10,6},{11,7},{4,8},{5,9},{14,10},{15,11},... | collective-permute-start | bytes 786440 | tf_op jit(solution)/shard_map/ppermute | solution.py:322
  7.8 5.5 %collective-permute-start.3 = (bf16[512,256]{1,0:T(8,128)(2,1)S(1)}, bf16[512,256]{1,0:T(8,128)(2,1)S(1)}, u32[]{:S(2)}, u32[]{:S(2)}) collective-permute-start(bf16[512,256]{1,0:T(8,128)(2,1)S(1)} %get-tuple-element.22), channel_id=1, source_target_pairs={{0,1},{1,0},{2,3},{3,2},{4,5},{5,4},{6,7},{7,6},{8,9},{9,8},{10,11... | collective-permute-start | bytes 786440 | tf_op jit(solution)/shard_map/ppermute | solution.py:25
  13.3 2.6 %collective-permute-start.1 = (bf16[512,256]{1,0:T(8,128)(2,1)S(1)}, bf16[512,256]{1,0:T(8,128)(2,1)S(1)}, u32[]{:S(2)}, u32[]{:S(2)}) collective-permute-start(bf16[512,256]{1,0:T(8,128)(2,1)S(1)} %collective-permute-done.halo), channel_id=1, source_target_pairs={{0,1},{1,0},{2,3},{3,2},{4,5},{5,4},{6,7},{7,6},{8,9},{9,8},{10,11... | collective-permute-start | bytes 786440 | tf_op jit(solution)/shard_map/ppermute | solution.py:25
  13.4 9.5 %collective-permute-start.4 = (bf16[512,256]{1,0:T(8,128)(2,1)S(1)}, bf16[512,256]{1,0:T(8,128)(2,1)S(1)}, u32[]{:S(2)}, u32[]{:S(2)}) collective-permute-start(bf16[512,256]{1,0:T(8,128)(2,1)S(1)} %add_convert_fusion.2), channel_id=1, source_target_pairs={{0,2},{1,3},{2,0},{3,1},{4,6},{5,7},{6,4},{7,5},{8,10},{9,11},{10,... | collective-permute-start | bytes 786440 | tf_op jit(solution)/shard_map/ppermute | solution.py:25
  16.6 6.3 %collective-permute-start.2 = (bf16[512,256]{1,0:T(8,128)(2,1)S(1)}, bf16[512,256]{1,0:T(8,128)(2,1)S(1)}, u32[]{:S(2)}, u32[]{:S(2)}) collective-permute-start(bf16[512,256]{1,0:T(8,128)(2,1)S(1)} %get-tuple-element.20), channel_id=1, source_target_pairs={{0,1},{1,0},{2,3},{3,2},{4,5},{5,4},{6,7},{7,6},{8,9},{9,8},{10,11... | collective-permute-start | bytes 786440 | tf_op jit(solution)/shard_map/ppermute | solution.py:25
  23.0 8.2 %collective-permute-start.6 = (bf16[512,256]{1,0:T(8,128)(2,1)S(1)}, bf16[512,256]{1,0:T(8,128)(2,1)S(1)}, u32[]{:S(2)}, u32[]{:S(2)}) collective-permute-start(bf16[512,256]{1,0:T(8,128)(2,1)S(1)} %add_convert_fusion.1.near0.own), channel_id=1, source_target_pairs={{0,2},{1,3},{2,0},{3,1},{4,6},{5,7},{6,4},{7,5},{8,10},{9,11},{10,... | collective-permute-start | bytes 786440 | tf_op jit(solution)/shard_map/ppermute | solution.py:25
  31.2 9.1 %collective-permute-start.7 = (bf16[512,256]{1,0:T(8,128)(2,1)S(1)}, bf16[512,256]{1,0:T(8,128)(2,1)S(1)}, u32[]{:S(2)}, u32[]{:S(2)}) collective-permute-start(bf16[512,256]{1,0:T(8,128)(2,1)S(1)} %collective-permute-done.6.far), channel_id=1, source_target_pairs={{6,2},{7,3},{0,4},{1,5},{10,6},{11,7},{4,8},{5,9},{14,10},{15,11},... | collective-permute-start | bytes 786440 | tf_op jit(solution)/shard_map/ppermute | solution.py:322
  35.6 4.8 %collective-permute-start.5 = (bf16[512,256]{1,0:T(8,128)(2,1)S(1)}, bf16[512,256]{1,0:T(8,128)(2,1)S(1)}, u32[]{:S(2)}, u32[]{:S(2)}) collective-permute-start(bf16[512,256]{1,0:T(8,128)(2,1)S(1)} %add_convert_fusion.1.near0.own), channel_id=1, source_target_pairs={{0,1},{1,0},{2,3},{3,2},{4,5},{5,4},{6,7},{7,6},{8,9},{9,8},{10,11... | collective-permute-start | bytes 786440 | tf_op jit(solution)/shard_map/ppermute | solution.py:25
  35.6 4.7 %collective-permute-start.10 = (bf16[512,256]{1,0:T(8,128)(2,1)S(1)}, bf16[512,256]{1,0:T(8,128)(2,1)S(1)}, u32[]{:S(2)}, u32[]{:S(2)}) collective-permute-start(bf16[512,256]{1,0:T(8,128)(2,1)S(1)} %collective-permute-done.6.far), channel_id=1, source_target_pairs={{0,1},{1,0},{2,3},{3,2},{4,5},{5,4},{6,7},{7,6},{8,9},{9,8},{10,11... | collective-permute-start | bytes 786440 | tf_op jit(solution)/shard_map/ppermute | solution.py:25
  40.3 1.5 %collective-permute-start.8 = (bf16[512,256]{1,0:T(8,128)(2,1)S(1)}, bf16[512,256]{1,0:T(8,128)(2,1)S(1)}, u32[]{:S(2)}, u32[]{:S(2)}) collective-permute-start(bf16[512,256]{1,0:T(8,128)(2,1)S(1)} %collective-permute-done.7.halo), channel_id=1, source_target_pairs={{0,1},{1,0},{2,3},{3,2},{4,5},{5,4},{6,7},{7,6},{8,9},{9,8},{10,11... | collective-permute-start | bytes 786440 | tf_op jit(solution)/shard_map/ppermute | solution.py:25
  41.0 1.7 %collective-permute-start.11 = (bf16[512,256]{1,0:T(8,128)(2,1)S(1)}, bf16[512,256]{1,0:T(8,128)(2,1)S(1)}, u32[]{:S(2)}, u32[]{:S(2)}) collective-permute-start(bf16[512,256]{1,0:T(8,128)(2,1)S(1)} %get-tuple-element.26), channel_id=1, source_target_pairs={{0,1},{1,0},{2,3},{3,2},{4,5},{5,4},{6,7},{7,6},{8,9},{9,8},{10,11... | collective-permute-start | bytes 786440 | tf_op jit(solution)/shard_map/ppermute | solution.py:25
  42.5 2.3 %collective-permute-start.9 = (bf16[512,256]{1,0:T(8,128)(2,1)S(1)}, bf16[512,256]{1,0:T(8,128)(2,1)S(1)}, u32[]{:S(2)}, u32[]{:S(2)}) collective-permute-start(bf16[512,256]{1,0:T(8,128)(2,1)S(1)} %get-tuple-element.24), channel_id=1, source_target_pairs={{0,1},{1,0},{2,3},{3,2},{4,5},{5,4},{6,7},{7,6},{8,9},{9,8},{10,11... | collective-permute-start | bytes 786440 | tf_op jit(solution)/shard_map/ppermute | solution.py:25
  42.8 8.8 %collective-permute-start.12 = (bf16[512,256]{1,0:T(8,128)(2,1)S(1)}, bf16[512,256]{1,0:T(8,128)(2,1)S(1)}, u32[]{:S(2)}, u32[]{:S(2)}) collective-permute-start(bf16[512,256]{1,0:T(8,128)(2,1)S(1)} %add_convert_fusion), channel_id=1, source_target_pairs={{0,2},{1,3},{2,0},{3,1},{4,6},{5,7},{6,4},{7,5},{8,10},{9,11},{10,... | collective-permute-start | bytes 786440 | tf_op jit(solution)/shard_map/ppermute | solution.py:25
  52.4 1.3 %collective-permute-start.13 = (f32[136,128]{1,0:T(8,128)S(1)}, f32[136,128]{1,0:T(8,128)S(1)}, u32[]{:S(2)}, u32[]{:S(2)}) collective-permute-start(f32[136,128]{1,0:T(8,128)S(1)} %get-tuple-element.28), channel_id=1, source_target_pairs={{0,1},{1,0},{2,3},{3,2},{4,5},{5,4},{6,7},{7,6},{8,9},{9,8},{10,11... | collective-permute-start | bytes 208904 | tf_op jit(solution)/shard_map/ppermute | solution.py:25
  53.7 4.4 %collective-permute-start.14 = (f32[136,128]{1,0:T(8,128)S(1)}, f32[136,128]{1,0:T(8,128)S(1)}, u32[]{:S(2)}, u32[]{:S(2)}) collective-permute-start(f32[136,128]{1,0:T(8,128)S(1)} %add.31), channel_id=1, source_target_pairs={{0,2},{1,3},{2,0},{3,1},{4,6},{5,7},{6,4},{7,5},{8,10},{9,11},{10,... | collective-permute-start | bytes 208904 | tf_op jit(solution)/shard_map/ppermute | solution.py:25
  58.1 5.0 %collective-permute-start.15 = (f32[136,128]{1,0:T(8,128)S(1)}, f32[136,128]{1,0:T(8,128)S(1)}, u32[]{:S(2)}, u32[]{:S(2)}) collective-permute-start(f32[136,128]{1,0:T(8,128)S(1)} %add.32), channel_id=1, source_target_pairs={{0,4},{4,0},{8,12},{12,8},{16,20},{20,16},{24,28},{28,24},{1,5},{5... | collective-permute-start | bytes 208904 | tf_op jit(solution)/shard_map/ppermute | solution.py:25
  63.1 4.7 %collective-permute-start.16 = (f32[136,128]{1,0:T(8,128)S(1)}, f32[136,128]{1,0:T(8,128)S(1)}, u32[]{:S(2)}, u32[]{:S(2)}) collective-permute-start(f32[136,128]{1,0:T(8,128)S(1)} %add.33), channel_id=1, source_target_pairs={{0,8},{4,12},{8,0},{12,4},{16,24},{20,28},{24,16},{28,20},{1,9},{5... | collective-permute-start | bytes 208904 | tf_op jit(solution)/shard_map/ppermute | solution.py:25
  67.8 6.8 %collective-permute-start.17 = (f32[136,128]{1,0:T(8,128)S(1)}, f32[136,128]{1,0:T(8,128)S(1)}, u32[]{:S(2)}, u32[]{:S(2)}) collective-permute-start(f32[136,128]{1,0:T(8,128)S(1)} %add.34), channel_id=1, source_target_pairs={{0,16},{4,20},{8,24},{12,28},{16,0},{20,4},{24,8},{28,12},{1,17},{... | collective-permute-start | bytes 208904 | tf_op jit(solution)/shard_map/ppermute | solution.py:25
  74.7 1.3 %collective-permute-start.18 = (f32[136,128]{1,0:T(8,128)S(1)}, f32[136,128]{1,0:T(8,128)S(1)}, u32[]{:S(2)}, u32[]{:S(2)}) collective-permute-start(f32[136,128]{1,0:T(8,128)S(1)} %add.35.mine), channel_id=1, source_target_pairs={{0,1},{1,0},{2,3},{3,2},{4,5},{5,4},{6,7},{7,6},{8,9},{9,8},{10,11... | collective-permute-start | bytes 208904 | tf_op jit(solution)/shard_map/ppermute | solution.py:25
where the time goes:
time: 87.3 us; the launch traced here: 87.2 us
  waiting for transfers between devices  41.9 us (48%)
  starting transfers between devices  28.1 us (32%)
  Pallas kernels  16.1 us (18%)
    ppermute x17, waiting for transfers between devices, flip(): return lax.ppermute(array, axis, [(i, i ^ bit) for i in range(count)])  32.2 us
    ppermute x17, starting transfers between devices, flip(): return lax.ppermute(array, axis, [(i, i ^ bit) for i in range(count)])  18.9 us
    pallas_call x1, Pallas kernels, factor_and_basis(): pl.pallas_call(functools.partial(factor_kernel, scale_root), out_shape=(j...  11.2 us
    ppermute x2, waiting for transfers between devices, halo_step(): return lax.ppermute(send, ('rows', 'band'), pairs)  9.64 us
    ppermute x2, starting transfers between devices, halo_step(): return lax.ppermute(send, ('rows', 'band'), pairs)  9.24 us
    pallas_call x4, Pallas kernels, product(): pl.pallas_call(kernel, out_shape=outputs, in_specs=[IN_HBM] * 2 if first...  4.23 us
  transfers between devices with their start and end apart: 19, of which 12 were waited for; matrix products, arithmetic and copies ran while one was open for 0% of the time, Pallas kernels for 2%

commit v1 on v0

--- a/solution.py
+++ b/solution.py
@@ -187,7 +187,11 @@
         }
         upper, scale = {}, []
         for p in pivots:
-            scale.append(lax.rsqrt(entry[p, p]))
+            if p % 2 == 0:
+                q = p + 1
+                root = lax.rsqrt(entry[p, p])
+                minor = entry[p, p] * entry[q, q] - entry[p, q] * entry[p, q]
+                scale += [root, lax.rsqrt(minor) * (entry[p, p] * root)]
             for t in range(p + 1, PIV):
                 upper[p, t] = entry[p, t] * scale[p]
             for t in range(p + 1, PIV):
@@ -219,7 +223,7 @@
     return jnp.concatenate(rows, 0)
 
 
-def factor_kernel(scale_root, mine, other, second, basis_ref, factor_ref, a_ref, b_ref, packed):
+def factor_kernel(scale_root, mine, other, second, basis_ref, factor_ref, packed):
     core = lax.axis_index("band") % 2
     part, mid = mine.shape
     size = 2 * mid
@@ -229,66 +233,89 @@
     turned = folded.T
     row = lax.broadcasted_iota(jnp.int32, (mid, mid), 0)
     column = lax.broadcasted_iota(jnp.int32, (mid, mid), 1)
-    a_ref[0:mid, 0:mid] = jnp.where(column >= row, folded, turned)
-    a_ref[0:mid, mid:size] = packed[0:mid, :]
-    diagonal = jnp.broadcast_to(packed[size : size + 1, :], (mid, mid))
-    a_ref[mid:size, mid:size] = jnp.where(
-        column < row, folded, jnp.where(column > row, turned, diagonal)
+    eye = row == column
+    below = jnp.broadcast_to(packed[size : size + 1, :], (mid, mid))
+    top = jnp.where(column >= row, folded, turned)
+    low = jnp.where(column < row, folded, jnp.where(column > row, turned, below))
+
+    diagonal = jnp.concatenate(
+        [jnp.sum(jnp.where(eye, top, 0.0), axis=0, keepdims=True), packed[size : size + 1, :]], 1
     )
-    a_ref[mid:size, 0:mid] = jnp.zeros((mid, mid), F32)
-    row_id = lax.broadcasted_iota(jnp.int32, (size, size), 0)
-    col_id = lax.broadcasted_iota(jnp.int32, (size, size), 1)
-    b_ref[...] = jnp.where(row_id == col_id, 1.0, 0.0).astype(F32)
-    factor_ref[...] = jnp.zeros_like(factor_ref)
+    root = lax.rsqrt(diagonal)
+
+    def as_column(values):
+        spread = jnp.where(eye, jnp.broadcast_to(values, (mid, mid)), 0.0)
+        return jnp.sum(spread, axis=1, keepdims=True)
+
+    top = jnp.concatenate([top, packed[0:mid, :]], 1) * root * as_column(root[:, :mid])
+    low = low * root[:, mid:] * as_column(root[:, mid:])
+    scaled = second[...] * (root * scale_root)
+    length = diagonal * root * (1.0 / scale_root)
+
     lane = lax.broadcasted_iota(jnp.int32, (NB, 128), 1)
-    row = lax.broadcasted_iota(jnp.int32, (NB, 128), 0)
+    line = lax.broadcasted_iota(jnp.int32, (NB, 128), 0)
     over_rows = (((0,), (0,)), ((), ()))
-    for first in range(0, size, NB):
-        after = first + NB
-        low = (first // 128) * 128
-        shift = first - low
-        block = a_ref[first:after, low : low + 128]
+
+    def times(a, b, dims=(((1,), (0,)), ((), ()))):
+        return lax.dot_general(a, b, dims, precision=HIGHEST, preferred_element_type=F32)
+
+    def widen(value, width, before=0):
+        parts = [value]
+        if before:
+            parts.insert(0, jnp.zeros((NB, before), F32))
+        after = width - before - value.shape[1]
+        if after:
+            parts.append(jnp.zeros((NB, after), F32))
+        return jnp.concatenate(parts, 1) if len(parts) > 1 else value
+
+    count = size // NB
+    start = [k * NB // 128 * 128 for k in range(count)]
+    ahead = [
+        top[k * NB : (k + 1) * NB, :] if start[k] == 0 else low[k * NB - mid : (k + 1) * NB - mid, :]
+        for k in range(count)
+    ]
+    behind = [None] * count
+    inverse = []
+    for k in range(count):
+        shift = k * NB - start[k]
+        block = ahead[k][:, :128]
         if shift:
             block = pltpu.roll(block, 128 - shift, 1)
-        block = jnp.where(lane < NB, block, jnp.where(lane - NB == row, 1.0, 0.0))
-        block = factor_block(block)
-        diagonal = jnp.where((lane < NB) & (lane >= row), block, 0.0)
+        block = factor_block(jnp.where(lane < NB, block, jnp.where(lane - NB == line, 1.0, 0.0)))
+        upper = jnp.where((lane < NB) & (lane >= line), block, 0.0)
+        lower = jnp.where(lane <= line, pltpu.roll(block, 128 - NB, 1), 0.0)[:, :NB]
         if shift:
-            diagonal = pltpu.roll(diagonal, shift, 1)
-        solve = jnp.where(lane <= row, pltpu.roll(block, 128 - NB, 1), 0.0)[:, :NB]
-        high = low + 128
-        right = jnp.dot(
-            solve, a_ref[first:after, low:size], precision=HIGHEST, preferred_element_type=F32
-        )
-        column = lax.broadcasted_iota(jnp.int32, right.shape, 1) + low
-        right = jnp.where(column >= after, right, 0.0)
-        left = jnp.dot(
-            solve, b_ref[first:after, 0:high], precision=HIGHEST, preferred_element_type=F32
-        )
-        if size > high:
-            diagonal = jnp.concatenate([diagonal, jnp.zeros((NB, size - high), F32)], 1)
-        factor_ref[first:after, low:size] = (right + diagonal) * (1.0 / scale_root)
-        b_ref[first:after, 0:high] = left
-        if after < size:
-            edge = (after // 128) * 128
-            ahead = right[:, edge - low :]
-            on_a = lax.dot_general(
-                ahead, ahead, over_rows, precision=HIGHEST, preferred_element_type=F32
-            )
-            on_b = lax.dot_general(
-                ahead, left, over_rows, precision=HIGHEST, preferred_element_type=F32
-            )
-            skip = after - edge
-            a_ref[after:size, edge:size] -= on_a[skip:, :]
-            b_ref[after:size, 0:high] -= on_b[skip:, :]
-    basis = lax.dot_general(
-        second[...],
-        b_ref[...],
-        (((1,), (1,)), ((), ())),
-        precision=HIGHEST,
-        preferred_element_type=F32,
-    )
-    basis_ref[...] = (basis * scale_root).astype(BF16)
+            upper = pltpu.roll(upper, shift, 1)
+        width = size - start[k]
+        upper = widen(upper, width)
+        if k + 1 < count:
+            right = times(lower, ahead[k])
+            place_of = lax.broadcasted_iota(jnp.int32, (NB, width), 1) + start[k]
+            right = jnp.where(place_of >= (k + 1) * NB, right, 0.0)
+            upper = upper + right
+            for i in range(k + 1, count):
+                at = i * NB - start[k]
+                ahead[i] = ahead[i] - times(
+                    right[:, at : at + NB], right[:, start[i] - start[k] :], over_rows
+                )
+        rows = slice(k * NB, (k + 1) * NB)
+        if start[k]:
+            factor_ref[rows, 0 : start[k]] = jnp.zeros((NB, start[k]), F32)
+        factor_ref[rows, start[k] :] = upper * length[:, start[k] :]
+        reach = start[k] + 128
+        own = widen(lower, 128)
+        if shift:
+            own = pltpu.roll(own, shift, 1)
+        left = widen(own, reach, start[k])
+        if behind[k] is not None:
+            left = left + times(lower, widen(behind[k], reach))
+        inverse.append(widen(left, size))
+        for i in range(k + 1, count):
+            at = i * NB - start[k]
+            change = times(right[:, at : at + NB], left, over_rows)
+            behind[i] = -change if behind[i] is None else widen(behind[i], reach) - change
+    basis = times(scaled, jnp.concatenate(inverse, 0), (((1,), (1,)), ((), ())))
+    basis_ref[...] = basis.astype(BF16)
 
 
 def factor_and_basis(mine, other, second, scale_root):
@@ -302,8 +329,6 @@
         in_specs=[VMEM] * 3,
         out_specs=(VMEM, VMEM),
         scratch_shapes=[
-            pltpu.VMEM((size, size), F32),
-            pltpu.VMEM((size, size), F32),
             pltpu.VMEM((size + 16, size // 2), F32),
         ],
         name="factor_kernel",
@@ -324,6 +349,15 @@
 
 def inner_step(halo):
     return flip(halo, "band", 1)
+
+
+def doubling_steps(slabs, bands):
+    levels = [2] + [bit * bands for bit in (1 << i for i in range(slabs.bit_length() - 1))]
+    turn = len(levels) // 2
+    orders = (levels, levels[turn:] + levels[:turn])
+    return [
+        [(d, d ^ orders[d % 2][step]) for d in range(slabs * bands)] for step in range(len(levels))
+    ]
 
 
 def add16(*parts):
@@ -358,11 +392,8 @@
 
     second, mine, other = gram(keep, near, far)
     mine = mine + flip(other, "band", 1)
-    mine = mine + flip(mine, "band", 2)
-    bit = 1
-    while bit < slabs:
-        mine = mine + flip(mine, "rows", bit)
-        bit *= 2
+    for pairs in doubling_steps(slabs, lax.axis_size("band")):
+        mine = mine + lax.ppermute(mine, ("rows", "band"), pairs)
     other = flip(mine, "band", 1)
     return factor_and_basis(mine, other, second, scale_root)
 

time: 87.3 us -> 85.6 us (0.981)
    ppermute x17 -> x13, starting transfers between devices: 18.9 us -> 8.16 us  [flip(): return lax.ppermute(array, axis, [(i, i ^ bit) for i in range(count)])]
    ppermute x17 -> x13, waiting for transfers between devices: 32.2 us -> 22.1 us  [flip(): return lax.ppermute(array, axis, [(i, i ^ bit) for i in range(count)])]
    ppermute x0 -> x4, starting transfers between devices: none -> 9.99 us  [per_device(): mine = mine + lax.ppermute(mine, ('rows', 'band'), pairs)]
    ppermute x0 -> x4, waiting for transfers between devices: none -> 9.44 us  [per_device(): mine = mine + lax.ppermute(mine, ('rows', 'band'), pairs)]
where the time goes in v1:
time: 85.6 us; the launch traced here: 85.4 us
  waiting for transfers between devices  41.1 us (48%)
  starting transfers between devices  27.4 us (32%)
  Pallas kernels  15.9 us (19%)
    ppermute x13, waiting for transfers between devices, flip(): return lax.ppermute(array, axis, [(i, i ^ bit) for i in range(count)])  22.1 us
    pallas_call x1, Pallas kernels, factor_and_basis(): pl.pallas_call(functools.partial(factor_kernel, scale_root), out_shape=(j...  10.9 us
    ppermute x4, starting transfers between devices, per_device(): mine = mine + lax.ppermute(mine, ('rows', 'band'), pairs)  9.99 us
    ppermute x2, waiting for transfers between devices, halo_step(): return lax.ppermute(send, ('rows', 'band'), pairs)  9.64 us
    ppermute x4, waiting for transfers between devices, per_device(): mine = mine + lax.ppermute(mine, ('rows', 'band'), pairs)  9.44 us
    ppermute x2, starting transfers between devices, halo_step(): return lax.ppermute(send, ('rows', 'band'), pairs)  9.24 us
    ppermute x13, starting transfers between devices, flip(): return lax.ppermute(array, axis, [(i, i ^ bit) for i in range(count)])  8.16 us
    pallas_call x4, Pallas kernels, product(): pl.pallas_call(kernel, out_shape=outputs, in_specs=[IN_HBM] * 2 if first...  4.23 us
  transfers between devices with their start and end apart: 19, of which 12 were waited for; matrix products, arithmetic and copies ran while one was open for 0% of the time, Pallas kernels for 2%

profile of v1, /device:TPU:0, one launch (start us, length us, event | category | flops | bytes accessed | tf_op | source)
XLA Modules:
  0.0 85.4 jit_solution(955231711786214155)
XLA Ops:
  0.6 2.2 %shard_map.41 = (bf16[512,256]{1,0:T(8,128)(2,1)S(1)}, bf16[512,256]{1,0:T(8,128)(2,1)S(1)}, bf16[512,256]{1,0:T(8,128)(2,1)S(1)}, bf16[2048,640]{1,0:T(8,128)(2,1)S(1)}, bf16[2048,256]{1,0:T(8,128)(2,1)S(1)}) custom-call(bf16[2048,640]{1,0:T(8,128)(2,1)} %coupling.1, bf16[2048,256]{1,0:T(8,128)(2,1)} %slab.1), custom_call_target="tpu_custom_call" | custom-call | flops 335544320 | bytes 1310720 | tf_op jit(solution)/shard_map/pallas_call | solution.py:115
  2.9 4.9 %collective-permute-start = (bf16[512,256]{1,0:T(8,128)(2,1)S(1)}, bf16[512,256]{1,0:T(8,128)(2,1)S(1)}, u32[]{:S(2)}, u32[]{:S(2)}) collective-permute-start(bf16[512,256]{1,0:T(8,128)(2,1)S(1)} %get-tuple-element.18), channel_id=1, source_target_pairs={{6,2},{7,3},{0,4},{1,5},{10,6},{11,7},{4,8},{5,9},{14,10},{15,11},... | collective-permute-start | bytes 786440 | tf_op jit(solution)/shard_map/ppermute | solution.py:347
  7.9 5.5 %collective-permute-done.halo = bf16[512,256]{1,0:T(8,128)(2,1)S(1)} collective-permute-done((bf16[512,256]{1,0:T(8,128)(2,1)S(1)}, bf16[512,256]{1,0:T(8,128)(2,1)S(1)}, u32[]{:S(2)}, u32[]{:S(2)}) %collective-permute-start) | collective-permute-done | bytes 262176 | tf_op jit(solution)/shard_map/ppermute | solution.py:347
  13.4 2.5 %collective-permute-start.4 = (bf16[512,256]{1,0:T(8,128)(2,1)S(1)}, bf16[512,256]{1,0:T(8,128)(2,1)S(1)}, u32[]{:S(2)}, u32[]{:S(2)}) collective-permute-start(bf16[512,256]{1,0:T(8,128)(2,1)S(1)} %add_convert_fusion.2), channel_id=1, source_target_pairs={{0,2},{1,3},{2,0},{3,1},{4,6},{5,7},{6,4},{7,5},{8,10},{9,11},{10,... | collective-permute-start | bytes 786440 | tf_op jit(solution)/shard_map/ppermute | solution.py:25
  15.9 0.7 shard_map.42
  16.6 0.3 collective-permute-start.2
  16.9 6.0 %collective-permute-done.4 = bf16[512,256]{1,0:T(8,128)(2,1)S(1)} collective-permute-done((bf16[512,256]{1,0:T(8,128)(2,1)S(1)}, bf16[512,256]{1,0:T(8,128)(2,1)S(1)}, u32[]{:S(2)}, u32[]{:S(2)}) %collective-permute-start.4) | collective-permute-done | bytes 262176 | tf_op jit(solution)/shard_map/ppermute | solution.py:25
  22.9 0.1 add_convert_fusion.1.near0.own
  23.0 1.8 %collective-permute-start.6 = (bf16[512,256]{1,0:T(8,128)(2,1)S(1)}, bf16[512,256]{1,0:T(8,128)(2,1)S(1)}, u32[]{:S(2)}, u32[]{:S(2)}) collective-permute-start(bf16[512,256]{1,0:T(8,128)(2,1)S(1)} %add_convert_fusion.1.near0.own), channel_id=1, source_target_pairs={{0,2},{1,3},{2,0},{3,1},{4,6},{5,7},{6,4},{7,5},{8,10},{9,11},{10,... | collective-permute-start | bytes 786440 | tf_op jit(solution)/shard_map/ppermute | solution.py:25
  24.8 6.4 %collective-permute-done.6.far = bf16[512,256]{1,0:T(8,128)(2,1)S(1)} collective-permute-done((bf16[512,256]{1,0:T(8,128)(2,1)S(1)}, bf16[512,256]{1,0:T(8,128)(2,1)S(1)}, u32[]{:S(2)}, u32[]{:S(2)}) %collective-permute-start.6) | collective-permute-done | bytes 262176 | tf_op jit(solution)/shard_map/ppermute | solution.py:25
  31.2 4.3 %collective-permute-start.7 = (bf16[512,256]{1,0:T(8,128)(2,1)S(1)}, bf16[512,256]{1,0:T(8,128)(2,1)S(1)}, u32[]{:S(2)}, u32[]{:S(2)}) collective-permute-start(bf16[512,256]{1,0:T(8,128)(2,1)S(1)} %collective-permute-done.6.far), channel_id=1, source_target_pairs={{6,2},{7,3},{0,4},{1,5},{10,6},{11,7},{4,8},{5,9},{14,10},{15,11},... | collective-permute-start | bytes 786440 | tf_op jit(solution)/shard_map/ppermute | solution.py:347
  35.6 0.5 collective-permute-start.10
  36.1 4.2 %collective-permute-done.7.halo = bf16[512,256]{1,0:T(8,128)(2,1)S(1)} collective-permute-done((bf16[512,256]{1,0:T(8,128)(2,1)S(1)}, bf16[512,256]{1,0:T(8,128)(2,1)S(1)}, u32[]{:S(2)}, u32[]{:S(2)}) %collective-permute-start.7) | collective-permute-done | bytes 262176 | tf_op jit(solution)/shard_map/ppermute | solution.py:347
  40.3 0.7 shard_map.44
  41.0 0.6 collective-permute-start.11
  41.6 0.3 collective-permute-done.8.halo2
  41.9 0.7 shard_map.43
  42.5 0.2 collective-permute-start.9
  42.8 2.0 %collective-permute-start.12 = (bf16[512,256]{1,0:T(8,128)(2,1)S(1)}, bf16[512,256]{1,0:T(8,128)(2,1)S(1)}, u32[]{:S(2)}, u32[]{:S(2)}) collective-permute-start(bf16[512,256]{1,0:T(8,128)(2,1)S(1)} %add_convert_fusion), channel_id=1, source_target_pairs={{0,2},{1,3},{2,0},{3,1},{4,6},{5,7},{6,4},{7,5},{8,10},{9,11},{10,... | collective-permute-start | bytes 786440 | tf_op jit(solution)/shard_map/ppermute | solution.py:25
  44.8 6.8 %collective-permute-done.12.far = bf16[512,256]{1,0:T(8,128)(2,1)S(1)} collective-permute-done((bf16[512,256]{1,0:T(8,128)(2,1)S(1)}, bf16[512,256]{1,0:T(8,128)(2,1)S(1)}, u32[]{:S(2)}, u32[]{:S(2)}) %collective-permute-start.12) | collective-permute-done | bytes 262176 | tf_op jit(solution)/shard_map/ppermute | solution.py:25
  51.6 0.7 gram_kernel.1
  52.4 1.2 %collective-permute-done.13 = f32[136,128]{1,0:T(8,128)S(1)} collective-permute-done((f32[136,128]{1,0:T(8,128)S(1)}, f32[136,128]{1,0:T(8,128)S(1)}, u32[]{:S(2)}, u32[]{:S(2)}) %collective-permute-start.13) | collective-permute-done | bytes 69664 | tf_op jit(solution)/shard_map/ppermute | solution.py:25
  53.7 1.8 %collective-permute-start.14 = (f32[136,128]{1,0:T(8,128)S(1)}, f32[136,128]{1,0:T(8,128)S(1)}, u32[]{:S(2)}, u32[]{:S(2)}) collective-permute-start(f32[136,128]{1,0:T(8,128)S(1)} %add.31), channel_id=1, source_target_pairs={{0,2},{1,9},{2,0},{3,11},{4,6},{5,13},{6,4},{7,15},{8,10},{9,1},{1... | collective-permute-start | bytes 208904 | tf_op jit(solution)/shard_map/ppermute | solution.py:396
  55.5 2.6 %collective-permute-done.14 = f32[136,128]{1,0:T(8,128)S(1)} collective-permute-done((f32[136,128]{1,0:T(8,128)S(1)}, f32[136,128]{1,0:T(8,128)S(1)}, u32[]{:S(2)}, u32[]{:S(2)}) %collective-permute-start.14) | collective-permute-done | bytes 69664 | tf_op jit(solution)/shard_map/ppermute | solution.py:396
  58.1 2.7 %collective-permute-start.15 = (f32[136,128]{1,0:T(8,128)S(1)}, f32[136,128]{1,0:T(8,128)S(1)}, u32[]{:S(2)}, u32[]{:S(2)}) collective-permute-start(f32[136,128]{1,0:T(8,128)S(1)} %add.32), channel_id=1, source_target_pairs={{0,4},{1,17},{2,6},{3,19},{4,0},{5,21},{6,2},{7,23},{8,12},{9,25},... | collective-permute-start | bytes 208904 | tf_op jit(solution)/shard_map/ppermute | solution.py:396
  60.8 2.3 %collective-permute-done.15 = f32[136,128]{1,0:T(8,128)S(1)} collective-permute-done((f32[136,128]{1,0:T(8,128)S(1)}, f32[136,128]{1,0:T(8,128)S(1)}, u32[]{:S(2)}, u32[]{:S(2)}) %collective-permute-start.15) | collective-permute-done | bytes 69664 | tf_op jit(solution)/shard_map/ppermute | solution.py:396
  63.1 2.4 %collective-permute-start.16 = (f32[136,128]{1,0:T(8,128)S(1)}, f32[136,128]{1,0:T(8,128)S(1)}, u32[]{:S(2)}, u32[]{:S(2)}) collective-permute-start(f32[136,128]{1,0:T(8,128)S(1)} %add.33), channel_id=1, source_target_pairs={{0,8},{1,3},{2,10},{3,1},{4,12},{5,7},{6,14},{7,5},{8,0},{9,11},{1... | collective-permute-start | bytes 208904 | tf_op jit(solution)/shard_map/ppermute | solution.py:396
  65.5 2.3 %collective-permute-done.16 = f32[136,128]{1,0:T(8,128)S(1)} collective-permute-done((f32[136,128]{1,0:T(8,128)S(1)}, f32[136,128]{1,0:T(8,128)S(1)}, u32[]{:S(2)}, u32[]{:S(2)}) %collective-permute-start.16) | collective-permute-done | bytes 69664 | tf_op jit(solution)/shard_map/ppermute | solution.py:396
  67.8 3.1 %collective-permute-start.17 = (f32[136,128]{1,0:T(8,128)S(1)}, f32[136,128]{1,0:T(8,128)S(1)}, u32[]{:S(2)}, u32[]{:S(2)}) collective-permute-start(f32[136,128]{1,0:T(8,128)S(1)} %add.34), channel_id=1, source_target_pairs={{0,16},{1,5},{2,18},{3,7},{4,20},{5,1},{6,22},{7,3},{8,24},{9,13},... | collective-permute-start | bytes 208904 | tf_op jit(solution)/shard_map/ppermute | solution.py:396
  70.9 2.3 %collective-permute-done.17 = f32[136,128]{1,0:T(8,128)S(1)} collective-permute-done((f32[136,128]{1,0:T(8,128)S(1)}, f32[136,128]{1,0:T(8,128)S(1)}, u32[]{:S(2)}, u32[]{:S(2)}) %collective-permute-start.17) | collective-permute-done | bytes 69664 | tf_op jit(solution)/shard_map/ppermute | solution.py:396
  73.3 1.2 %collective-permute-done.18.other = f32[136,128]{1,0:T(8,128)S(1)} collective-permute-done((f32[136,128]{1,0:T(8,128)S(1)}, f32[136,128]{1,0:T(8,128)S(1)}, u32[]{:S(2)}, u32[]{:S(2)}) %collective-permute-start.18) | collective-permute-done | bytes 69664 | tf_op jit(solution)/shard_map/ppermute | solution.py:25
  74.5 10.9 %factor_kernel.1 = (bf16[512,256]{1,0:T(8,128)(2,1)}, f32[256,256]{1,0:T(8,128)}) custom-call(f32[136,128]{1,0:T(8,128)S(1)} %add.35.mine, f32[136,128]{1,0:T(8,128)S(1)} %collective-permute-done.18.other, f32[512,256]{1,0:T(8,128)S(1)} %get-tuple-element.29.second), custom_call_target="tpu_custom_call" | custom-call | tf_op jit(solution)/shard_map/factor_kernel/pallas_call | solution.py:323
  (20 shorter events, 0.5 us)
Async XLA Ops:
  2.9 10.5 %collective-permute-start = (bf16[512,256]{1,0:T(8,128)(2,1)S(1)}, bf16[512,256]{1,0:T(8,128)(2,1)S(1)}, u32[]{:S(2)}, u32[]{:S(2)}) collective-permute-start(bf16[512,256]{1,0:T(8,128)(2,1)S(1)} %get-tuple-element.18), channel_id=1, source_target_pairs={{6,2},{7,3},{0,4},{1,5},{10,6},{11,7},{4,8},{5,9},{14,10},{15,11},... | collective-permute-start | bytes 786440 | tf_op jit(solution)/shard_map/ppermute | solution.py:347
  7.8 5.5 %collective-permute-start.3 = (bf16[512,256]{1,0:T(8,128)(2,1)S(1)}, bf16[512,256]{1,0:T(8,128)(2,1)S(1)}, u32[]{:S(2)}, u32[]{:S(2)}) collective-permute-start(bf16[512,256]{1,0:T(8,128)(2,1)S(1)} %get-tuple-element.22), channel_id=1, source_target_pairs={{0,1},{1,0},{2,3},{3,2},{4,5},{5,4},{6,7},{7,6},{8,9},{9,8},{10,11... | collective-permute-start | bytes 786440 | tf_op jit(solution)/shard_map/ppermute | solution.py:25
  13.3 2.6 %collective-permute-start.1 = (bf16[512,256]{1,0:T(8,128)(2,1)S(1)}, bf16[512,256]{1,0:T(8,128)(2,1)S(1)}, u32[]{:S(2)}, u32[]{:S(2)}) collective-permute-start(bf16[512,256]{1,0:T(8,128)(2,1)S(1)} %collective-permute-done.halo), channel_id=1, source_target_pairs={{0,1},{1,0},{2,3},{3,2},{4,5},{5,4},{6,7},{7,6},{8,9},{9,8},{10,11... | collective-permute-start | bytes 786440 | tf_op jit(solution)/shard_map/ppermute | solution.py:25
  13.4 9.5 %collective-permute-start.4 = (bf16[512,256]{1,0:T(8,128)(2,1)S(1)}, bf16[512,256]{1,0:T(8,128)(2,1)S(1)}, u32[]{:S(2)}, u32[]{:S(2)}) collective-permute-start(bf16[512,256]{1,0:T(8,128)(2,1)S(1)} %add_convert_fusion.2), channel_id=1, source_target_pairs={{0,2},{1,3},{2,0},{3,1},{4,6},{5,7},{6,4},{7,5},{8,10},{9,11},{10,... | collective-permute-start | bytes 786440 | tf_op jit(solution)/shard_map/ppermute | solution.py:25
  16.6 6.3 %collective-permute-start.2 = (bf16[512,256]{1,0:T(8,128)(2,1)S(1)}, bf16[512,256]{1,0:T(8,128)(2,1)S(1)}, u32[]{:S(2)}, u32[]{:S(2)}) collective-permute-start(bf16[512,256]{1,0:T(8,128)(2,1)S(1)} %get-tuple-element.20), channel_id=1, source_target_pairs={{0,1},{1,0},{2,3},{3,2},{4,5},{5,4},{6,7},{7,6},{8,9},{9,8},{10,11... | collective-permute-start | bytes 786440 | tf_op jit(solution)/shard_map/ppermute | solution.py:25
  23.0 8.2 %collective-permute-start.6 = (bf16[512,256]{1,0:T(8,128)(2,1)S(1)}, bf16[512,256]{1,0:T(8,128)(2,1)S(1)}, u32[]{:S(2)}, u32[]{:S(2)}) collective-permute-start(bf16[512,256]{1,0:T(8,128)(2,1)S(1)} %add_convert_fusion.1.near0.own), channel_id=1, source_target_pairs={{0,2},{1,3},{2,0},{3,1},{4,6},{5,7},{6,4},{7,5},{8,10},{9,11},{10,... | collective-permute-start | bytes 786440 | tf_op jit(solution)/shard_map/ppermute | solution.py:25
  31.2 9.1 %collective-permute-start.7 = (bf16[512,256]{1,0:T(8,128)(2,1)S(1)}, bf16[512,256]{1,0:T(8,128)(2,1)S(1)}, u32[]{:S(2)}, u32[]{:S(2)}) collective-permute-start(bf16[512,256]{1,0:T(8,128)(2,1)S(1)} %collective-permute-done.6.far), channel_id=1, source_target_pairs={{6,2},{7,3},{0,4},{1,5},{10,6},{11,7},{4,8},{5,9},{14,10},{15,11},... | collective-permute-start | bytes 786440 | tf_op jit(solution)/shard_map/ppermute | solution.py:347
  35.6 4.8 %collective-permute-start.5 = (bf16[512,256]{1,0:T(8,128)(2,1)S(1)}, bf16[512,256]{1,0:T(8,128)(2,1)S(1)}, u32[]{:S(2)}, u32[]{:S(2)}) collective-permute-start(bf16[512,256]{1,0:T(8,128)(2,1)S(1)} %add_convert_fusion.1.near0.own), channel_id=1, source_target_pairs={{0,1},{1,0},{2,3},{3,2},{4,5},{5,4},{6,7},{7,6},{8,9},{9,8},{10,11... | collective-permute-start | bytes 786440 | tf_op jit(solution)/shard_map/ppermute | solution.py:25
  35.6 4.7 %collective-permute-start.10 = (bf16[512,256]{1,0:T(8,128)(2,1)S(1)}, bf16[512,256]{1,0:T(8,128)(2,1)S(1)}, u32[]{:S(2)}, u32[]{:S(2)}) collective-permute-start(bf16[512,256]{1,0:T(8,128)(2,1)S(1)} %collective-permute-done.6.far), channel_id=1, source_target_pairs={{0,1},{1,0},{2,3},{3,2},{4,5},{5,4},{6,7},{7,6},{8,9},{9,8},{10,11... | collective-permute-start | bytes 786440 | tf_op jit(solution)/shard_map/ppermute | solution.py:25
  40.3 1.5 %collective-permute-start.8 = (bf16[512,256]{1,0:T(8,128)(2,1)S(1)}, bf16[512,256]{1,0:T(8,128)(2,1)S(1)}, u32[]{:S(2)}, u32[]{:S(2)}) collective-permute-start(bf16[512,256]{1,0:T(8,128)(2,1)S(1)} %collective-permute-done.7.halo), channel_id=1, source_target_pairs={{0,1},{1,0},{2,3},{3,2},{4,5},{5,4},{6,7},{7,6},{8,9},{9,8},{10,11... | collective-permute-start | bytes 786440 | tf_op jit(solution)/shard_map/ppermute | solution.py:25
  41.0 1.7 %collective-permute-start.11 = (bf16[512,256]{1,0:T(8,128)(2,1)S(1)}, bf16[512,256]{1,0:T(8,128)(2,1)S(1)}, u32[]{:S(2)}, u32[]{:S(2)}) collective-permute-start(bf16[512,256]{1,0:T(8,128)(2,1)S(1)} %get-tuple-element.26), channel_id=1, source_target_pairs={{0,1},{1,0},{2,3},{3,2},{4,5},{5,4},{6,7},{7,6},{8,9},{9,8},{10,11... | collective-permute-start | bytes 786440 | tf_op jit(solution)/shard_map/ppermute | solution.py:25
  42.5 2.3 %collective-permute-start.9 = (bf16[512,256]{1,0:T(8,128)(2,1)S(1)}, bf16[512,256]{1,0:T(8,128)(2,1)S(1)}, u32[]{:S(2)}, u32[]{:S(2)}) collective-permute-start(bf16[512,256]{1,0:T(8,128)(2,1)S(1)} %get-tuple-element.24), channel_id=1, source_target_pairs={{0,1},{1,0},{2,3},{3,2},{4,5},{5,4},{6,7},{7,6},{8,9},{9,8},{10,11... | collective-permute-start | bytes 786440 | tf_op jit(solution)/shard_map/ppermute | solution.py:25
  42.8 8.8 %collective-permute-start.12 = (bf16[512,256]{1,0:T(8,128)(2,1)S(1)}, bf16[512,256]{1,0:T(8,128)(2,1)S(1)}, u32[]{:S(2)}, u32[]{:S(2)}) collective-permute-start(bf16[512,256]{1,0:T(8,128)(2,1)S(1)} %add_convert_fusion), channel_id=1, source_target_pairs={{0,2},{1,3},{2,0},{3,1},{4,6},{5,7},{6,4},{7,5},{8,10},{9,11},{10,... | collective-permute-start | bytes 786440 | tf_op jit(solution)/shard_map/ppermute | solution.py:25
  52.4 1.3 %collective-permute-start.13 = (f32[136,128]{1,0:T(8,128)S(1)}, f32[136,128]{1,0:T(8,128)S(1)}, u32[]{:S(2)}, u32[]{:S(2)}) collective-permute-start(f32[136,128]{1,0:T(8,128)S(1)} %get-tuple-element.28), channel_id=1, source_target_pairs={{0,1},{1,0},{2,3},{3,2},{4,5},{5,4},{6,7},{7,6},{8,9},{9,8},{10,11... | collective-permute-start | bytes 208904 | tf_op jit(solution)/shard_map/ppermute | solution.py:25
  53.7 4.4 %collective-permute-start.14 = (f32[136,128]{1,0:T(8,128)S(1)}, f32[136,128]{1,0:T(8,128)S(1)}, u32[]{:S(2)}, u32[]{:S(2)}) collective-permute-start(f32[136,128]{1,0:T(8,128)S(1)} %add.31), channel_id=1, source_target_pairs={{0,2},{1,9},{2,0},{3,11},{4,6},{5,13},{6,4},{7,15},{8,10},{9,1},{1... | collective-permute-start | bytes 208904 | tf_op jit(solution)/shard_map/ppermute | solution.py:396
  58.1 5.0 %collective-permute-start.15 = (f32[136,128]{1,0:T(8,128)S(1)}, f32[136,128]{1,0:T(8,128)S(1)}, u32[]{:S(2)}, u32[]{:S(2)}) collective-permute-start(f32[136,128]{1,0:T(8,128)S(1)} %add.32), channel_id=1, source_target_pairs={{0,4},{1,17},{2,6},{3,19},{4,0},{5,21},{6,2},{7,23},{8,12},{9,25},... | collective-permute-start | bytes 208904 | tf_op jit(solution)/shard_map/ppermute | solution.py:396
  63.1 4.7 %collective-permute-start.16 = (f32[136,128]{1,0:T(8,128)S(1)}, f32[136,128]{1,0:T(8,128)S(1)}, u32[]{:S(2)}, u32[]{:S(2)}) collective-permute-start(f32[136,128]{1,0:T(8,128)S(1)} %add.33), channel_id=1, source_target_pairs={{0,8},{1,3},{2,10},{3,1},{4,12},{5,7},{6,14},{7,5},{8,0},{9,11},{1... | collective-permute-start | bytes 208904 | tf_op jit(solution)/shard_map/ppermute | solution.py:396
  67.8 5.4 %collective-permute-start.17 = (f32[136,128]{1,0:T(8,128)S(1)}, f32[136,128]{1,0:T(8,128)S(1)}, u32[]{:S(2)}, u32[]{:S(2)}) collective-permute-start(f32[136,128]{1,0:T(8,128)S(1)} %add.34), channel_id=1, source_target_pairs={{0,16},{1,5},{2,18},{3,7},{4,20},{5,1},{6,22},{7,3},{8,24},{9,13},... | collective-permute-start | bytes 208904 | tf_op jit(solution)/shard_map/ppermute | solution.py:396
  73.2 1.3 %collective-permute-start.18 = (f32[136,128]{1,0:T(8,128)S(1)}, f32[136,128]{1,0:T(8,128)S(1)}, u32[]{:S(2)}, u32[]{:S(2)}) collective-permute-start(f32[136,128]{1,0:T(8,128)S(1)} %add.35.mine), channel_id=1, source_target_pairs={{0,1},{1,0},{2,3},{3,2},{4,5},{5,4},{6,7},{7,6},{8,9},{9,8},{10,11... | collective-permute-start | bytes 208904 | tf_op jit(solution)/shard_map/ppermute | solution.py:25

commit v2 on v1

--- a/solution.py
+++ b/solution.py
@@ -46,8 +46,8 @@
         ).astype(BF16)
 
 
-def first_kernel(coupling, slab, keep_ref, send_ref, edge_ref, coupling_ref, slab_ref, sems):
-    _, half, core = place()
+def first_kernel(coupling, slab, keep_ref, send_ref, coupling_ref, slab_ref, sems):
+    _, half, _ = place()
     base = pl.multiple_of((1 - half) * HB, HB)
     late = pl.multiple_of(half * HB, HB)
     loads = [pltpu.make_async_copy(slab, slab_ref, sems.at[0])]
@@ -59,7 +59,6 @@
     for load in loads:
         load.start()
     loads[0].wait()
-    edge_ref[...] = slab_ref[tile_rows(base, core), :]
     loads[1].wait()
     run_tiles(base, coupling_ref, slab_ref, keep_ref, send_ref)
     loads[2].wait()
@@ -105,7 +104,7 @@
     outputs = [jax.ShapeDtypeStruct((TB, columns), BF16)] * 2
     scratch = [pltpu.VMEM((2 * HB, columns), BF16)]
     if first:
-        outputs += [outputs[0]] + [
+        outputs += [
             jax.ShapeDtypeStruct(array.shape, BF16) for array in (coupling, fields[0])
         ]
         scratch = [pltpu.SemaphoreType.DMA((3,))]
@@ -181,7 +180,9 @@
             for p in pivots
         ]
         entry = {
-            (p, t): jnp.broadcast_to(column[p][own][at + t : at + t + 1, :], shape)
+            (p, t): jnp.take_along_axis(
+                column[p][own], jnp.full(shape, at + t, jnp.int32), axis=0
+            )
             for p in pivots
             for t in range(p, PIV)
         }
@@ -371,9 +372,11 @@
     slabs = lax.axis_size("rows")
     scale_root = math.sqrt(sketch.shape[0] * slabs)
 
-    keep, send, edge, coupling, sketch = product(first_kernel, coupling, sketch)
+    band = lax.axis_index("band")
+    edge_at = (1 - band // 2) * HB + band % 2 * TB
+    halo = halo_step(lax.dynamic_slice_in_dim(sketch, edge_at, TB, 0), False)
+    keep, send, coupling, sketch = product(first_kernel, coupling, sketch)
     near = flip(send, "band", 1)
-    halo = halo_step(edge, False)
     far = flip(add16(keep, near), "band", 2)
     halo2 = inner_step(halo)
     keep, send = product(late_kernel_slab, coupling, sketch, halo, halo2)

time: 85.6 us -> 81.8 us (0.956)
  Pallas kernels: 15.9 us -> 13.3 us
  waiting for transfers between devices: 41.1 us -> 38.9 us
  local copies, waits for them, and re-layouts: 0 us -> 0.97 us
    pallas_call x1, Pallas kernels: 10.9 us -> 8.32 us  [factor_and_basis(): pl.pallas_call(functools.partial(factor_kernel, scale_root), out_shape=(j...]
    ppermute x2, waiting for transfers between devices: 9.64 us -> 7.39 us  [halo_step(): return lax.ppermute(send, ('rows', 'band'), pairs)]
    dynamic_slice x0 -> x1, local copies, waits for them, and re-layouts: none -> 0.97 us  [per_device(): halo = halo_step(lax.dynamic_slice_in_dim(sketch, edge_at, TB, 0), False)]
  transfers between devices with their start and end apart: 19 -> 19, of which waited for: 12 -> 12; matrix products, arithmetic and copies ran while one was open for 0% -> 0% of each run, Pallas kernels for 2% -> 5%
where the time goes in v2:
time: 81.8 us; the launch traced here: 81.6 us
  waiting for transfers between devices  38.9 us (48%)
  starting transfers between devices  27.4 us (33%)
  Pallas kernels  13.3 us (16%)
  local copies, waits for them, and re-layouts  0.97 us (1%)
    ppermute x13, waiting for transfers between devices, flip(): return lax.ppermute(array, axis, [(i, i ^ bit) for i in range(count)])  22.1 us
    ppermute x4, starting transfers between devices, per_device(): mine = mine + lax.ppermute(mine, ('rows', 'band'), pairs)  9.99 us
    ppermute x4, waiting for transfers between devices, per_device(): mine = mine + lax.ppermute(mine, ('rows', 'band'), pairs)  9.44 us
    ppermute x2, starting transfers between devices, halo_step(): return lax.ppermute(send, ('rows', 'band'), pairs)  9.24 us
    pallas_call x1, Pallas kernels, factor_and_basis(): pl.pallas_call(functools.partial(factor_kernel, scale_root), out_shape=(j...  8.32 us
    ppermute x13, starting transfers between devices, flip(): return lax.ppermute(array, axis, [(i, i ^ bit) for i in range(count)])  8.16 us
    ppermute x2, waiting for transfers between devices, halo_step(): return lax.ppermute(send, ('rows', 'band'), pairs)  7.39 us
    pallas_call x4, Pallas kernels, product(): pl.pallas_call(kernel, out_shape=outputs, in_specs=[IN_HBM] * 2 if first...  4.23 us
  transfers between devices with their start and end apart: 19, of which 12 were waited for; matrix products, arithmetic and copies ran while one was open for 0% of the time, Pallas kernels for 5%

profile of v2, /device:TPU:0, one launch (start us, length us, event | category | flops | bytes accessed | tf_op | source)
XLA Modules:
  0.0 81.6 jit_solution(15359329284963526269)
XLA Ops:
  0.7 1.0 %constant_dynamic-slice_fusion = bf16[512,256]{1,0:T(8,128)(2,1)S(1)} fusion(bf16[2048,256]{1,0:T(8,128)(2,1)} %slab.1, s32[]{:T(128)S(6)} %select_n.16), kind=kLoop, calls=%fused_computation.3 | loop fusion | bytes 524292 | tf_op jit(solution)/shard_map/dynamic_slice | solution.py:377
  1.6 4.9 %collective-permute-start = (bf16[512,256]{1,0:T(8,128)(2,1)S(1)}, bf16[512,256]{1,0:T(8,128)(2,1)S(1)}, u32[]{:S(2)}, u32[]{:S(2)}) collective-permute-start(bf16[512,256]{1,0:T(8,128)(2,1)S(1)} %constant_dynamic-slice_fusion), channel_id=1, source_target_pairs={{6,2},{7,3},{0,4},{1,5},{10,6},{11,7},{4,8},{5,9},{14,10},{15,11},... | collective-permute-start | bytes 786440 | tf_op jit(solution)/shard_map/ppermute | solution.py:348
  6.6 2.2 %shard_map.41 = (bf16[512,256]{1,0:T(8,128)(2,1)S(1)}, bf16[512,256]{1,0:T(8,128)(2,1)S(1)}, bf16[2048,640]{1,0:T(8,128)(2,1)S(1)}, bf16[2048,256]{1,0:T(8,128)(2,1)S(1)}) custom-call(bf16[2048,640]{1,0:T(8,128)(2,1)} %coupling.1, bf16[2048,256]{1,0:T(8,128)(2,1)} %slab.1), custom_call_target="tpu_custom_call" | custom-call | flops 335544320 | bytes 1310720 | tf_op jit(solution)/shard_map/pallas_call | solution.py:114
  8.9 3.2 %collective-permute-done.halo = bf16[512,256]{1,0:T(8,128)(2,1)S(1)} collective-permute-done((bf16[512,256]{1,0:T(8,128)(2,1)S(1)}, bf16[512,256]{1,0:T(8,128)(2,1)S(1)}, u32[]{:S(2)}, u32[]{:S(2)}) %collective-permute-start) | collective-permute-done | bytes 262176 | tf_op jit(solution)/shard_map/ppermute | solution.py:348
  12.2 2.5 %collective-permute-start.4 = (bf16[512,256]{1,0:T(8,128)(2,1)S(1)}, bf16[512,256]{1,0:T(8,128)(2,1)S(1)}, u32[]{:S(2)}, u32[]{:S(2)}) collective-permute-start(bf16[512,256]{1,0:T(8,128)(2,1)S(1)} %add_convert_fusion.2), channel_id=1, source_target_pairs={{0,2},{1,3},{2,0},{3,1},{4,6},{5,7},{6,4},{7,5},{8,10},{9,11},{10,... | collective-permute-start | bytes 786440 | tf_op jit(solution)/shard_map/ppermute | solution.py:25
  14.7 0.7 shard_map.42
  15.4 0.3 collective-permute-start.2
  15.6 6.0 %collective-permute-done.4 = bf16[512,256]{1,0:T(8,128)(2,1)S(1)} collective-permute-done((bf16[512,256]{1,0:T(8,128)(2,1)S(1)}, bf16[512,256]{1,0:T(8,128)(2,1)S(1)}, u32[]{:S(2)}, u32[]{:S(2)}) %collective-permute-start.4) | collective-permute-done | bytes 262176 | tf_op jit(solution)/shard_map/ppermute | solution.py:25
  21.8 1.8 %collective-permute-start.6 = (bf16[512,256]{1,0:T(8,128)(2,1)S(1)}, bf16[512,256]{1,0:T(8,128)(2,1)S(1)}, u32[]{:S(2)}, u32[]{:S(2)}) collective-permute-start(bf16[512,256]{1,0:T(8,128)(2,1)S(1)} %add_convert_fusion.1.near0.own), channel_id=1, source_target_pairs={{0,2},{1,3},{2,0},{3,1},{4,6},{5,7},{6,4},{7,5},{8,10},{9,11},{10,... | collective-permute-start | bytes 786440 | tf_op jit(solution)/shard_map/ppermute | solution.py:25
  23.6 6.4 %collective-permute-done.6.far = bf16[512,256]{1,0:T(8,128)(2,1)S(1)} collective-permute-done((bf16[512,256]{1,0:T(8,128)(2,1)S(1)}, bf16[512,256]{1,0:T(8,128)(2,1)S(1)}, u32[]{:S(2)}, u32[]{:S(2)}) %collective-permute-start.6) | collective-permute-done | bytes 262176 | tf_op jit(solution)/shard_map/ppermute | solution.py:25
  30.0 4.3 %collective-permute-start.7 = (bf16[512,256]{1,0:T(8,128)(2,1)S(1)}, bf16[512,256]{1,0:T(8,128)(2,1)S(1)}, u32[]{:S(2)}, u32[]{:S(2)}) collective-permute-start(bf16[512,256]{1,0:T(8,128)(2,1)S(1)} %collective-permute-done.6.far), channel_id=1, source_target_pairs={{6,2},{7,3},{0,4},{1,5},{10,6},{11,7},{4,8},{5,9},{14,10},{15,11},... | collective-permute-start | bytes 786440 | tf_op jit(solution)/shard_map/ppermute | solution.py:348
  34.4 0.5 collective-permute-start.10
  34.9 4.2 %collective-permute-done.7.halo = bf16[512,256]{1,0:T(8,128)(2,1)S(1)} collective-permute-done((bf16[512,256]{1,0:T(8,128)(2,1)S(1)}, bf16[512,256]{1,0:T(8,128)(2,1)S(1)}, u32[]{:S(2)}, u32[]{:S(2)}) %collective-permute-start.7) | collective-permute-done | bytes 262176 | tf_op jit(solution)/shard_map/ppermute | solution.py:348
  39.1 0.7 shard_map.44
  39.8 0.6 collective-permute-start.11
  40.3 0.3 collective-permute-done.8.halo2
  40.6 0.7 shard_map.43
  41.3 0.2 collective-permute-start.9
  41.6 2.0 %collective-permute-start.12 = (bf16[512,256]{1,0:T(8,128)(2,1)S(1)}, bf16[512,256]{1,0:T(8,128)(2,1)S(1)}, u32[]{:S(2)}, u32[]{:S(2)}) collective-permute-start(bf16[512,256]{1,0:T(8,128)(2,1)S(1)} %add_convert_fusion), channel_id=1, source_target_pairs={{0,2},{1,3},{2,0},{3,1},{4,6},{5,7},{6,4},{7,5},{8,10},{9,11},{10,... | collective-permute-start | bytes 786440 | tf_op jit(solution)/shard_map/ppermute | solution.py:25
  43.6 6.8 %collective-permute-done.12.far = bf16[512,256]{1,0:T(8,128)(2,1)S(1)} collective-permute-done((bf16[512,256]{1,0:T(8,128)(2,1)S(1)}, bf16[512,256]{1,0:T(8,128)(2,1)S(1)}, u32[]{:S(2)}, u32[]{:S(2)}) %collective-permute-start.12) | collective-permute-done | bytes 262176 | tf_op jit(solution)/shard_map/ppermute | solution.py:25
  50.4 0.7 gram_kernel.1
  51.2 1.2 %collective-permute-done.13 = f32[136,128]{1,0:T(8,128)S(1)} collective-permute-done((f32[136,128]{1,0:T(8,128)S(1)}, f32[136,128]{1,0:T(8,128)S(1)}, u32[]{:S(2)}, u32[]{:S(2)}) %collective-permute-start.13) | collective-permute-done | bytes 69664 | tf_op jit(solution)/shard_map/ppermute | solution.py:25
  52.4 1.8 %collective-permute-start.14 = (f32[136,128]{1,0:T(8,128)S(1)}, f32[136,128]{1,0:T(8,128)S(1)}, u32[]{:S(2)}, u32[]{:S(2)}) collective-permute-start(f32[136,128]{1,0:T(8,128)S(1)} %add.45), channel_id=1, source_target_pairs={{0,2},{1,9},{2,0},{3,11},{4,6},{5,13},{6,4},{7,15},{8,10},{9,1},{1... | collective-permute-start | bytes 208904 | tf_op jit(solution)/shard_map/ppermute | solution.py:399
  54.3 2.6 %collective-permute-done.14 = f32[136,128]{1,0:T(8,128)S(1)} collective-permute-done((f32[136,128]{1,0:T(8,128)S(1)}, f32[136,128]{1,0:T(8,128)S(1)}, u32[]{:S(2)}, u32[]{:S(2)}) %collective-permute-start.14) | collective-permute-done | bytes 69664 | tf_op jit(solution)/shard_map/ppermute | solution.py:399
  56.8 2.7 %collective-permute-start.15 = (f32[136,128]{1,0:T(8,128)S(1)}, f32[136,128]{1,0:T(8,128)S(1)}, u32[]{:S(2)}, u32[]{:S(2)}) collective-permute-start(f32[136,128]{1,0:T(8,128)S(1)} %add.46), channel_id=1, source_target_pairs={{0,4},{1,17},{2,6},{3,19},{4,0},{5,21},{6,2},{7,23},{8,12},{9,25},... | collective-permute-start | bytes 208904 | tf_op jit(solution)/shard_map/ppermute | solution.py:399
  59.5 2.3 %collective-permute-done.15 = f32[136,128]{1,0:T(8,128)S(1)} collective-permute-done((f32[136,128]{1,0:T(8,128)S(1)}, f32[136,128]{1,0:T(8,128)S(1)}, u32[]{:S(2)}, u32[]{:S(2)}) %collective-permute-start.15) | collective-permute-done | bytes 69664 | tf_op jit(solution)/shard_map/ppermute | solution.py:399
  61.8 2.4 %collective-permute-start.16 = (f32[136,128]{1,0:T(8,128)S(1)}, f32[136,128]{1,0:T(8,128)S(1)}, u32[]{:S(2)}, u32[]{:S(2)}) collective-permute-start(f32[136,128]{1,0:T(8,128)S(1)} %add.47), channel_id=1, source_target_pairs={{0,8},{1,3},{2,10},{3,1},{4,12},{5,7},{6,14},{7,5},{8,0},{9,11},{1... | collective-permute-start | bytes 208904 | tf_op jit(solution)/shard_map/ppermute | solution.py:399
  64.2 2.3 %collective-permute-done.16 = f32[136,128]{1,0:T(8,128)S(1)} collective-permute-done((f32[136,128]{1,0:T(8,128)S(1)}, f32[136,128]{1,0:T(8,128)S(1)}, u32[]{:S(2)}, u32[]{:S(2)}) %collective-permute-start.16) | collective-permute-done | bytes 69664 | tf_op jit(solution)/shard_map/ppermute | solution.py:399
  66.5 3.1 %collective-permute-start.17 = (f32[136,128]{1,0:T(8,128)S(1)}, f32[136,128]{1,0:T(8,128)S(1)}, u32[]{:S(2)}, u32[]{:S(2)}) collective-permute-start(f32[136,128]{1,0:T(8,128)S(1)} %add.48), channel_id=1, source_target_pairs={{0,16},{1,5},{2,18},{3,7},{4,20},{5,1},{6,22},{7,3},{8,24},{9,13},... | collective-permute-start | bytes 208904 | tf_op jit(solution)/shard_map/ppermute | solution.py:399
  69.6 2.3 %collective-permute-done.17 = f32[136,128]{1,0:T(8,128)S(1)} collective-permute-done((f32[136,128]{1,0:T(8,128)S(1)}, f32[136,128]{1,0:T(8,128)S(1)}, u32[]{:S(2)}, u32[]{:S(2)}) %collective-permute-start.17) | collective-permute-done | bytes 69664 | tf_op jit(solution)/shard_map/ppermute | solution.py:399
  72.0 1.2 %collective-permute-done.18.other = f32[136,128]{1,0:T(8,128)S(1)} collective-permute-done((f32[136,128]{1,0:T(8,128)S(1)}, f32[136,128]{1,0:T(8,128)S(1)}, u32[]{:S(2)}, u32[]{:S(2)}) %collective-permute-start.18) | collective-permute-done | bytes 69664 | tf_op jit(solution)/shard_map/ppermute | solution.py:25
  73.3 8.3 %factor_kernel.1 = (bf16[512,256]{1,0:T(8,128)(2,1)}, f32[256,256]{1,0:T(8,128)}) custom-call(f32[136,128]{1,0:T(8,128)S(1)} %add.49.mine, f32[136,128]{1,0:T(8,128)S(1)} %collective-permute-done.18.other, f32[512,256]{1,0:T(8,128)S(1)} %get-tuple-element.27.second), custom_call_target="tpu_custom_call" | custom-call | tf_op jit(solution)/shard_map/factor_kernel/pallas_call | solution.py:324
  (21 shorter events, 0.6 us)
Async XLA Ops:
  1.6 10.5 %collective-permute-start = (bf16[512,256]{1,0:T(8,128)(2,1)S(1)}, bf16[512,256]{1,0:T(8,128)(2,1)S(1)}, u32[]{:S(2)}, u32[]{:S(2)}) collective-permute-start(bf16[512,256]{1,0:T(8,128)(2,1)S(1)} %constant_dynamic-slice_fusion), channel_id=1, source_target_pairs={{6,2},{7,3},{0,4},{1,5},{10,6},{11,7},{4,8},{5,9},{14,10},{15,11},... | collective-permute-start | bytes 786440 | tf_op jit(solution)/shard_map/ppermute | solution.py:348
  8.8 3.3 %collective-permute-start.3 = (bf16[512,256]{1,0:T(8,128)(2,1)S(1)}, bf16[512,256]{1,0:T(8,128)(2,1)S(1)}, u32[]{:S(2)}, u32[]{:S(2)}) collective-permute-start(bf16[512,256]{1,0:T(8,128)(2,1)S(1)} %get-tuple-element.20), channel_id=1, source_target_pairs={{0,1},{1,0},{2,3},{3,2},{4,5},{5,4},{6,7},{7,6},{8,9},{9,8},{10,11... | collective-permute-start | bytes 786440 | tf_op jit(solution)/shard_map/ppermute | solution.py:25
  12.1 2.6 %collective-permute-start.1 = (bf16[512,256]{1,0:T(8,128)(2,1)S(1)}, bf16[512,256]{1,0:T(8,128)(2,1)S(1)}, u32[]{:S(2)}, u32[]{:S(2)}) collective-permute-start(bf16[512,256]{1,0:T(8,128)(2,1)S(1)} %collective-permute-done.halo), channel_id=1, source_target_pairs={{0,1},{1,0},{2,3},{3,2},{4,5},{5,4},{6,7},{7,6},{8,9},{9,8},{10,11... | collective-permute-start | bytes 786440 | tf_op jit(solution)/shard_map/ppermute | solution.py:25
  12.2 9.5 %collective-permute-start.4 = (bf16[512,256]{1,0:T(8,128)(2,1)S(1)}, bf16[512,256]{1,0:T(8,128)(2,1)S(1)}, u32[]{:S(2)}, u32[]{:S(2)}) collective-permute-start(bf16[512,256]{1,0:T(8,128)(2,1)S(1)} %add_convert_fusion.2), channel_id=1, source_target_pairs={{0,2},{1,3},{2,0},{3,1},{4,6},{5,7},{6,4},{7,5},{8,10},{9,11},{10,... | collective-permute-start | bytes 786440 | tf_op jit(solution)/shard_map/ppermute | solution.py:25
  15.4 6.3 %collective-permute-start.2 = (bf16[512,256]{1,0:T(8,128)(2,1)S(1)}, bf16[512,256]{1,0:T(8,128)(2,1)S(1)}, u32[]{:S(2)}, u32[]{:S(2)}) collective-permute-start(bf16[512,256]{1,0:T(8,128)(2,1)S(1)} %get-tuple-element.18), channel_id=1, source_target_pairs={{0,1},{1,0},{2,3},{3,2},{4,5},{5,4},{6,7},{7,6},{8,9},{9,8},{10,11... | collective-permute-start | bytes 786440 | tf_op jit(solution)/shard_map/ppermute | solution.py:25
  21.8 8.2 %collective-permute-start.6 = (bf16[512,256]{1,0:T(8,128)(2,1)S(1)}, bf16[512,256]{1,0:T(8,128)(2,1)S(1)}, u32[]{:S(2)}, u32[]{:S(2)}) collective-permute-start(bf16[512,256]{1,0:T(8,128)(2,1)S(1)} %add_convert_fusion.1.near0.own), channel_id=1, source_target_pairs={{0,2},{1,3},{2,0},{3,1},{4,6},{5,7},{6,4},{7,5},{8,10},{9,11},{10,... | collective-permute-start | bytes 786440 | tf_op jit(solution)/shard_map/ppermute | solution.py:25
  30.0 9.1 %collective-permute-start.7 = (bf16[512,256]{1,0:T(8,128)(2,1)S(1)}, bf16[512,256]{1,0:T(8,128)(2,1)S(1)}, u32[]{:S(2)}, u32[]{:S(2)}) collective-permute-start(bf16[512,256]{1,0:T(8,128)(2,1)S(1)} %collective-permute-done.6.far), channel_id=1, source_target_pairs={{6,2},{7,3},{0,4},{1,5},{10,6},{11,7},{4,8},{5,9},{14,10},{15,11},... | collective-permute-start | bytes 786440 | tf_op jit(solution)/shard_map/ppermute | solution.py:348
  34.3 4.8 %collective-permute-start.5 = (bf16[512,256]{1,0:T(8,128)(2,1)S(1)}, bf16[512,256]{1,0:T(8,128)(2,1)S(1)}, u32[]{:S(2)}, u32[]{:S(2)}) collective-permute-start(bf16[512,256]{1,0:T(8,128)(2,1)S(1)} %add_convert_fusion.1.near0.own), channel_id=1, source_target_pairs={{0,1},{1,0},{2,3},{3,2},{4,5},{5,4},{6,7},{7,6},{8,9},{9,8},{10,11... | collective-permute-start | bytes 786440 | tf_op jit(solution)/shard_map/ppermute | solution.py:25
  34.4 4.7 %collective-permute-start.10 = (bf16[512,256]{1,0:T(8,128)(2,1)S(1)}, bf16[512,256]{1,0:T(8,128)(2,1)S(1)}, u32[]{:S(2)}, u32[]{:S(2)}) collective-permute-start(bf16[512,256]{1,0:T(8,128)(2,1)S(1)} %collective-permute-done.6.far), channel_id=1, source_target_pairs={{0,1},{1,0},{2,3},{3,2},{4,5},{5,4},{6,7},{7,6},{8,9},{9,8},{10,11... | collective-permute-start | bytes 786440 | tf_op jit(solution)/shard_map/ppermute | solution.py:25
  39.1 1.5 %collective-permute-start.8 = (bf16[512,256]{1,0:T(8,128)(2,1)S(1)}, bf16[512,256]{1,0:T(8,128)(2,1)S(1)}, u32[]{:S(2)}, u32[]{:S(2)}) collective-permute-start(bf16[512,256]{1,0:T(8,128)(2,1)S(1)} %collective-permute-done.7.halo), channel_id=1, source_target_pairs={{0,1},{1,0},{2,3},{3,2},{4,5},{5,4},{6,7},{7,6},{8,9},{9,8},{10,11... | collective-permute-start | bytes 786440 | tf_op jit(solution)/shard_map/ppermute | solution.py:25
  39.8 1.7 %collective-permute-start.11 = (bf16[512,256]{1,0:T(8,128)(2,1)S(1)}, bf16[512,256]{1,0:T(8,128)(2,1)S(1)}, u32[]{:S(2)}, u32[]{:S(2)}) collective-permute-start(bf16[512,256]{1,0:T(8,128)(2,1)S(1)} %get-tuple-element.24), channel_id=1, source_target_pairs={{0,1},{1,0},{2,3},{3,2},{4,5},{5,4},{6,7},{7,6},{8,9},{9,8},{10,11... | collective-permute-start | bytes 786440 | tf_op jit(solution)/shard_map/ppermute | solution.py:25
  41.3 2.3 %collective-permute-start.9 = (bf16[512,256]{1,0:T(8,128)(2,1)S(1)}, bf16[512,256]{1,0:T(8,128)(2,1)S(1)}, u32[]{:S(2)}, u32[]{:S(2)}) collective-permute-start(bf16[512,256]{1,0:T(8,128)(2,1)S(1)} %get-tuple-element.22), channel_id=1, source_target_pairs={{0,1},{1,0},{2,3},{3,2},{4,5},{5,4},{6,7},{7,6},{8,9},{9,8},{10,11... | collective-permute-start | bytes 786440 | tf_op jit(solution)/shard_map/ppermute | solution.py:25
  41.6 8.8 %collective-permute-start.12 = (bf16[512,256]{1,0:T(8,128)(2,1)S(1)}, bf16[512,256]{1,0:T(8,128)(2,1)S(1)}, u32[]{:S(2)}, u32[]{:S(2)}) collective-permute-start(bf16[512,256]{1,0:T(8,128)(2,1)S(1)} %add_convert_fusion), channel_id=1, source_target_pairs={{0,2},{1,3},{2,0},{3,1},{4,6},{5,7},{6,4},{7,5},{8,10},{9,11},{10,... | collective-permute-start | bytes 786440 | tf_op jit(solution)/shard_map/ppermute | solution.py:25
  51.1 1.3 %collective-permute-start.13 = (f32[136,128]{1,0:T(8,128)S(1)}, f32[136,128]{1,0:T(8,128)S(1)}, u32[]{:S(2)}, u32[]{:S(2)}) collective-permute-start(f32[136,128]{1,0:T(8,128)S(1)} %get-tuple-element.26), channel_id=1, source_target_pairs={{0,1},{1,0},{2,3},{3,2},{4,5},{5,4},{6,7},{7,6},{8,9},{9,8},{10,11... | collective-permute-start | bytes 208904 | tf_op jit(solution)/shard_map/ppermute | solution.py:25
  52.4 4.4 %collective-permute-start.14 = (f32[136,128]{1,0:T(8,128)S(1)}, f32[136,128]{1,0:T(8,128)S(1)}, u32[]{:S(2)}, u32[]{:S(2)}) collective-permute-start(f32[136,128]{1,0:T(8,128)S(1)} %add.45), channel_id=1, source_target_pairs={{0,2},{1,9},{2,0},{3,11},{4,6},{5,13},{6,4},{7,15},{8,10},{9,1},{1... | collective-permute-start | bytes 208904 | tf_op jit(solution)/shard_map/ppermute | solution.py:399
  56.8 5.0 %collective-permute-start.15 = (f32[136,128]{1,0:T(8,128)S(1)}, f32[136,128]{1,0:T(8,128)S(1)}, u32[]{:S(2)}, u32[]{:S(2)}) collective-permute-start(f32[136,128]{1,0:T(8,128)S(1)} %add.46), channel_id=1, source_target_pairs={{0,4},{1,17},{2,6},{3,19},{4,0},{5,21},{6,2},{7,23},{8,12},{9,25},... | collective-permute-start | bytes 208904 | tf_op jit(solution)/shard_map/ppermute | solution.py:399
  61.8 4.7 %collective-permute-start.16 = (f32[136,128]{1,0:T(8,128)S(1)}, f32[136,128]{1,0:T(8,128)S(1)}, u32[]{:S(2)}, u32[]{:S(2)}) collective-permute-start(f32[136,128]{1,0:T(8,128)S(1)} %add.47), channel_id=1, source_target_pairs={{0,8},{1,3},{2,10},{3,1},{4,12},{5,7},{6,14},{7,5},{8,0},{9,11},{1... | collective-permute-start | bytes 208904 | tf_op jit(solution)/shard_map/ppermute | solution.py:399
  66.5 5.4 %collective-permute-start.17 = (f32[136,128]{1,0:T(8,128)S(1)}, f32[136,128]{1,0:T(8,128)S(1)}, u32[]{:S(2)}, u32[]{:S(2)}) collective-permute-start(f32[136,128]{1,0:T(8,128)S(1)} %add.48), channel_id=1, source_target_pairs={{0,16},{1,5},{2,18},{3,7},{4,20},{5,1},{6,22},{7,3},{8,24},{9,13},... | collective-permute-start | bytes 208904 | tf_op jit(solution)/shard_map/ppermute | solution.py:399
  71.9 1.3 %collective-permute-start.18 = (f32[136,128]{1,0:T(8,128)S(1)}, f32[136,128]{1,0:T(8,128)S(1)}, u32[]{:S(2)}, u32[]{:S(2)}) collective-permute-start(f32[136,128]{1,0:T(8,128)S(1)} %add.49.mine), channel_id=1, source_target_pairs={{0,1},{1,0},{2,3},{3,2},{4,5},{5,4},{6,7},{7,6},{8,9},{9,8},{10,11... | collective-permute-start | bytes 208904 | tf_op jit(solution)/shard_map/ppermute | solution.py:25

commit v3 on v2

--- a/solution.py
+++ b/solution.py
@@ -44,6 +44,25 @@
             field[pl.ds(first, width), :],
             preferred_element_type=F32,
         ).astype(BF16)
+
+
+def edge_kernel(slab, edge_ref, sem):
+    _, half, core = place()
+    load = pltpu.make_async_copy(slab.at[tile_rows((1 - half) * HB, core), :], edge_ref, sem)
+    load.start()
+    load.wait()
+
+
+def edge_of(slab):
+    return pl.pallas_call(
+        edge_kernel,
+        out_shape=jax.ShapeDtypeStruct((TB, slab.shape[1]), BF16),
+        in_specs=[IN_HBM],
+        out_specs=VMEM,
+        scratch_shapes=[pltpu.SemaphoreType.DMA],
+        name="edge_kernel",
+        compiler_params=pltpu.CompilerParams(vmem_limit_bytes=1 << 20),
+    )(pltpu.with_memory_space_constraint(slab, pltpu.HBM))
 
 
 def first_kernel(coupling, slab, keep_ref, send_ref, coupling_ref, slab_ref, sems):
@@ -372,9 +391,7 @@
     slabs = lax.axis_size("rows")
     scale_root = math.sqrt(sketch.shape[0] * slabs)
 
-    band = lax.axis_index("band")
-    edge_at = (1 - band // 2) * HB + band % 2 * TB
-    halo = halo_step(lax.dynamic_slice_in_dim(sketch, edge_at, TB, 0), False)
+    halo = halo_step(edge_of(sketch), False)
     keep, send, coupling, sketch = product(first_kernel, coupling, sketch)
     near = flip(send, "band", 1)
     far = flip(add16(keep, near), "band", 2)

time: 81.8 us -> 81.8 us (level)
  local copies, waits for them, and re-layouts: 0.97 us -> 0 us
  Pallas kernels: 13.3 us -> 14.2 us
    pallas_call x0 -> x1, Pallas kernels: none -> 0.97 us  [edge_of(): pl.pallas_call(edge_kernel, out_shape=jax.ShapeDtypeStruct((TB, slab.shap...]
    dynamic_slice x1 -> x0, local copies, waits for them, and re-layouts: 0.97 us -> none  [per_device(): halo = halo_step(lax.dynamic_slice_in_dim(sketch, edge_at, TB, 0), False)]
where the time goes in v3:
time: 81.8 us; the launch traced here: 81.6 us
  waiting for transfers between devices  38.9 us (48%)
  starting transfers between devices  27.4 us (33%)
  Pallas kernels  14.2 us (17%)
    ppermute x13, waiting for transfers between devices, flip(): return lax.ppermute(array, axis, [(i, i ^ bit) for i in range(count)])  22.1 us
    ppermute x4, starting transfers between devices, per_device(): mine = mine + lax.ppermute(mine, ('rows', 'band'), pairs)  9.99 us
    ppermute x4, waiting for transfers between devices, per_device(): mine = mine + lax.ppermute(mine, ('rows', 'band'), pairs)  9.44 us
    ppermute x2, starting transfers between devices, halo_step(): return lax.ppermute(send, ('rows', 'band'), pairs)  9.24 us
    pallas_call x1, Pallas kernels, factor_and_basis(): pl.pallas_call(functools.partial(factor_kernel, scale_root), out_shape=(j...  8.32 us
    ppermute x13, starting transfers between devices, flip(): return lax.ppermute(array, axis, [(i, i ^ bit) for i in range(count)])  8.16 us
    ppermute x2, waiting for transfers between devices, halo_step(): return lax.ppermute(send, ('rows', 'band'), pairs)  7.39 us
    pallas_call x4, Pallas kernels, product(): pl.pallas_call(kernel, out_shape=outputs, in_specs=[IN_HBM] * 2 if first...  4.23 us
  transfers between devices with their start and end apart: 19, of which 12 were waited for; matrix products, arithmetic and copies ran while one was open for 0% of the time, Pallas kernels for 5%

profile of v3, /device:TPU:0, one launch (start us, length us, event | category | flops | bytes accessed | tf_op | source)
XLA Modules:
  0.0 81.6 jit_solution(16846651725237491852)
XLA Ops:
  0.6 1.0 %edge_kernel.1 = bf16[512,256]{1,0:T(8,128)(2,1)S(1)} custom-call(bf16[2048,256]{1,0:T(8,128)(2,1)} %slab.3), custom_call_target="tpu_custom_call" | custom-call | tf_op jit(solution)/shard_map/edge_kernel/pallas_call | solution.py:57
  1.6 4.9 %collective-permute-start = (bf16[512,256]{1,0:T(8,128)(2,1)S(1)}, bf16[512,256]{1,0:T(8,128)(2,1)S(1)}, u32[]{:S(2)}, u32[]{:S(2)}) collective-permute-start(bf16[512,256]{1,0:T(8,128)(2,1)S(1)} %edge_kernel.1), channel_id=1, source_target_pairs={{6,2},{7,3},{0,4},{1,5},{10,6},{11,7},{4,8},{5,9},{14,10},{15,11},... | collective-permute-start | bytes 786440 | tf_op jit(solution)/shard_map/ppermute | solution.py:367
  6.5 2.3 %shard_map.41 = (bf16[512,256]{1,0:T(8,128)(2,1)S(1)}, bf16[512,256]{1,0:T(8,128)(2,1)S(1)}, bf16[2048,640]{1,0:T(8,128)(2,1)S(1)}, bf16[2048,256]{1,0:T(8,128)(2,1)S(1)}) custom-call(bf16[2048,640]{1,0:T(8,128)(2,1)} %coupling.1, bf16[2048,256]{1,0:T(8,128)(2,1)} %slab.3), custom_call_target="tpu_custom_call" | custom-call | flops 335544320 | bytes 1310720 | tf_op jit(solution)/shard_map/pallas_call | solution.py:133
  8.9 3.2 %collective-permute-done.halo = bf16[512,256]{1,0:T(8,128)(2,1)S(1)} collective-permute-done((bf16[512,256]{1,0:T(8,128)(2,1)S(1)}, bf16[512,256]{1,0:T(8,128)(2,1)S(1)}, u32[]{:S(2)}, u32[]{:S(2)}) %collective-permute-start) | collective-permute-done | bytes 262176 | tf_op jit(solution)/shard_map/ppermute | solution.py:367
  12.1 2.5 %collective-permute-start.4 = (bf16[512,256]{1,0:T(8,128)(2,1)S(1)}, bf16[512,256]{1,0:T(8,128)(2,1)S(1)}, u32[]{:S(2)}, u32[]{:S(2)}) collective-permute-start(bf16[512,256]{1,0:T(8,128)(2,1)S(1)} %add_convert_fusion.2), channel_id=1, source_target_pairs={{0,2},{1,3},{2,0},{3,1},{4,6},{5,7},{6,4},{7,5},{8,10},{9,11},{10,... | collective-permute-start | bytes 786440 | tf_op jit(solution)/shard_map/ppermute | solution.py:25
  14.7 0.7 shard_map.42
  15.3 0.3 collective-permute-start.2
  15.6 6.0 %collective-permute-done.4 = bf16[512,256]{1,0:T(8,128)(2,1)S(1)} collective-permute-done((bf16[512,256]{1,0:T(8,128)(2,1)S(1)}, bf16[512,256]{1,0:T(8,128)(2,1)S(1)}, u32[]{:S(2)}, u32[]{:S(2)}) %collective-permute-start.4) | collective-permute-done | bytes 262176 | tf_op jit(solution)/shard_map/ppermute | solution.py:25
  21.7 1.8 %collective-permute-start.6 = (bf16[512,256]{1,0:T(8,128)(2,1)S(1)}, bf16[512,256]{1,0:T(8,128)(2,1)S(1)}, u32[]{:S(2)}, u32[]{:S(2)}) collective-permute-start(bf16[512,256]{1,0:T(8,128)(2,1)S(1)} %add_convert_fusion.1.near0.own), channel_id=1, source_target_pairs={{0,2},{1,3},{2,0},{3,1},{4,6},{5,7},{6,4},{7,5},{8,10},{9,11},{10,... | collective-permute-start | bytes 786440 | tf_op jit(solution)/shard_map/ppermute | solution.py:25
  23.6 6.4 %collective-permute-done.6.far = bf16[512,256]{1,0:T(8,128)(2,1)S(1)} collective-permute-done((bf16[512,256]{1,0:T(8,128)(2,1)S(1)}, bf16[512,256]{1,0:T(8,128)(2,1)S(1)}, u32[]{:S(2)}, u32[]{:S(2)}) %collective-permute-start.6) | collective-permute-done | bytes 262176 | tf_op jit(solution)/shard_map/ppermute | solution.py:25
  30.0 4.3 %collective-permute-start.7 = (bf16[512,256]{1,0:T(8,128)(2,1)S(1)}, bf16[512,256]{1,0:T(8,128)(2,1)S(1)}, u32[]{:S(2)}, u32[]{:S(2)}) collective-permute-start(bf16[512,256]{1,0:T(8,128)(2,1)S(1)} %collective-permute-done.6.far), channel_id=1, source_target_pairs={{6,2},{7,3},{0,4},{1,5},{10,6},{11,7},{4,8},{5,9},{14,10},{15,11},... | collective-permute-start | bytes 786440 | tf_op jit(solution)/shard_map/ppermute | solution.py:367
  34.4 0.5 collective-permute-start.10
  34.9 4.2 %collective-permute-done.7.halo = bf16[512,256]{1,0:T(8,128)(2,1)S(1)} collective-permute-done((bf16[512,256]{1,0:T(8,128)(2,1)S(1)}, bf16[512,256]{1,0:T(8,128)(2,1)S(1)}, u32[]{:S(2)}, u32[]{:S(2)}) %collective-permute-start.7) | collective-permute-done | bytes 262176 | tf_op jit(solution)/shard_map/ppermute | solution.py:367
  39.1 0.7 shard_map.44
  39.7 0.6 collective-permute-start.11
  40.3 0.3 collective-permute-done.8.halo2
  40.6 0.7 shard_map.43
  41.3 0.2 collective-permute-start.9
  41.5 2.0 %collective-permute-start.12 = (bf16[512,256]{1,0:T(8,128)(2,1)S(1)}, bf16[512,256]{1,0:T(8,128)(2,1)S(1)}, u32[]{:S(2)}, u32[]{:S(2)}) collective-permute-start(bf16[512,256]{1,0:T(8,128)(2,1)S(1)} %add_convert_fusion), channel_id=1, source_target_pairs={{0,2},{1,3},{2,0},{3,1},{4,6},{5,7},{6,4},{7,5},{8,10},{9,11},{10,... | collective-permute-start | bytes 786440 | tf_op jit(solution)/shard_map/ppermute | solution.py:25
  43.5 6.8 %collective-permute-done.12.far = bf16[512,256]{1,0:T(8,128)(2,1)S(1)} collective-permute-done((bf16[512,256]{1,0:T(8,128)(2,1)S(1)}, bf16[512,256]{1,0:T(8,128)(2,1)S(1)}, u32[]{:S(2)}, u32[]{:S(2)}) %collective-permute-start.12) | collective-permute-done | bytes 262176 | tf_op jit(solution)/shard_map/ppermute | solution.py:25
  50.4 0.7 gram_kernel.1
  51.2 1.2 %collective-permute-done.13 = f32[136,128]{1,0:T(8,128)S(1)} collective-permute-done((f32[136,128]{1,0:T(8,128)S(1)}, f32[136,128]{1,0:T(8,128)S(1)}, u32[]{:S(2)}, u32[]{:S(2)}) %collective-permute-start.13) | collective-permute-done | bytes 69664 | tf_op jit(solution)/shard_map/ppermute | solution.py:25
  52.4 1.8 %collective-permute-start.14 = (f32[136,128]{1,0:T(8,128)S(1)}, f32[136,128]{1,0:T(8,128)S(1)}, u32[]{:S(2)}, u32[]{:S(2)}) collective-permute-start(f32[136,128]{1,0:T(8,128)S(1)} %add.31), channel_id=1, source_target_pairs={{0,2},{1,9},{2,0},{3,11},{4,6},{5,13},{6,4},{7,15},{8,10},{9,1},{1... | collective-permute-start | bytes 208904 | tf_op jit(solution)/shard_map/ppermute | solution.py:416
  54.2 2.6 %collective-permute-done.14 = f32[136,128]{1,0:T(8,128)S(1)} collective-permute-done((f32[136,128]{1,0:T(8,128)S(1)}, f32[136,128]{1,0:T(8,128)S(1)}, u32[]{:S(2)}, u32[]{:S(2)}) %collective-permute-start.14) | collective-permute-done | bytes 69664 | tf_op jit(solution)/shard_map/ppermute | solution.py:416
  56.8 2.7 %collective-permute-start.15 = (f32[136,128]{1,0:T(8,128)S(1)}, f32[136,128]{1,0:T(8,128)S(1)}, u32[]{:S(2)}, u32[]{:S(2)}) collective-permute-start(f32[136,128]{1,0:T(8,128)S(1)} %add.32), channel_id=1, source_target_pairs={{0,4},{1,17},{2,6},{3,19},{4,0},{5,21},{6,2},{7,23},{8,12},{9,25},... | collective-permute-start | bytes 208904 | tf_op jit(solution)/shard_map/ppermute | solution.py:416
  59.5 2.3 %collective-permute-done.15 = f32[136,128]{1,0:T(8,128)S(1)} collective-permute-done((f32[136,128]{1,0:T(8,128)S(1)}, f32[136,128]{1,0:T(8,128)S(1)}, u32[]{:S(2)}, u32[]{:S(2)}) %collective-permute-start.15) | collective-permute-done | bytes 69664 | tf_op jit(solution)/shard_map/ppermute | solution.py:416
  61.8 2.4 %collective-permute-start.16 = (f32[136,128]{1,0:T(8,128)S(1)}, f32[136,128]{1,0:T(8,128)S(1)}, u32[]{:S(2)}, u32[]{:S(2)}) collective-permute-start(f32[136,128]{1,0:T(8,128)S(1)} %add.33), channel_id=1, source_target_pairs={{0,8},{1,3},{2,10},{3,1},{4,12},{5,7},{6,14},{7,5},{8,0},{9,11},{1... | collective-permute-start | bytes 208904 | tf_op jit(solution)/shard_map/ppermute | solution.py:416
  64.2 2.3 %collective-permute-done.16 = f32[136,128]{1,0:T(8,128)S(1)} collective-permute-done((f32[136,128]{1,0:T(8,128)S(1)}, f32[136,128]{1,0:T(8,128)S(1)}, u32[]{:S(2)}, u32[]{:S(2)}) %collective-permute-start.16) | collective-permute-done | bytes 69664 | tf_op jit(solution)/shard_map/ppermute | solution.py:416
  66.5 3.1 %collective-permute-start.17 = (f32[136,128]{1,0:T(8,128)S(1)}, f32[136,128]{1,0:T(8,128)S(1)}, u32[]{:S(2)}, u32[]{:S(2)}) collective-permute-start(f32[136,128]{1,0:T(8,128)S(1)} %add.34), channel_id=1, source_target_pairs={{0,16},{1,5},{2,18},{3,7},{4,20},{5,1},{6,22},{7,3},{8,24},{9,13},... | collective-permute-start | bytes 208904 | tf_op jit(solution)/shard_map/ppermute | solution.py:416
  69.6 2.3 %collective-permute-done.17 = f32[136,128]{1,0:T(8,128)S(1)} collective-permute-done((f32[136,128]{1,0:T(8,128)S(1)}, f32[136,128]{1,0:T(8,128)S(1)}, u32[]{:S(2)}, u32[]{:S(2)}) %collective-permute-start.17) | collective-permute-done | bytes 69664 | tf_op jit(solution)/shard_map/ppermute | solution.py:416
  72.0 1.2 %collective-permute-done.18.other = f32[136,128]{1,0:T(8,128)S(1)} collective-permute-done((f32[136,128]{1,0:T(8,128)S(1)}, f32[136,128]{1,0:T(8,128)S(1)}, u32[]{:S(2)}, u32[]{:S(2)}) %collective-permute-start.18) | collective-permute-done | bytes 69664 | tf_op jit(solution)/shard_map/ppermute | solution.py:25
  73.2 8.3 %factor_kernel.1 = (bf16[512,256]{1,0:T(8,128)(2,1)}, f32[256,256]{1,0:T(8,128)}) custom-call(f32[136,128]{1,0:T(8,128)S(1)} %add.35.mine, f32[136,128]{1,0:T(8,128)S(1)} %collective-permute-done.18.other, f32[512,256]{1,0:T(8,128)S(1)} %get-tuple-element.27.second), custom_call_target="tpu_custom_call" | custom-call | tf_op jit(solution)/shard_map/factor_kernel/pallas_call | solution.py:343
  (21 shorter events, 0.6 us)
Async XLA Ops:
  1.6 10.5 %collective-permute-start = (bf16[512,256]{1,0:T(8,128)(2,1)S(1)}, bf16[512,256]{1,0:T(8,128)(2,1)S(1)}, u32[]{:S(2)}, u32[]{:S(2)}) collective-permute-start(bf16[512,256]{1,0:T(8,128)(2,1)S(1)} %edge_kernel.1), channel_id=1, source_target_pairs={{6,2},{7,3},{0,4},{1,5},{10,6},{11,7},{4,8},{5,9},{14,10},{15,11},... | collective-permute-start | bytes 786440 | tf_op jit(solution)/shard_map/ppermute | solution.py:367
  8.8 3.3 %collective-permute-start.3 = (bf16[512,256]{1,0:T(8,128)(2,1)S(1)}, bf16[512,256]{1,0:T(8,128)(2,1)S(1)}, u32[]{:S(2)}, u32[]{:S(2)}) collective-permute-start(bf16[512,256]{1,0:T(8,128)(2,1)S(1)} %get-tuple-element.20), channel_id=1, source_target_pairs={{0,1},{1,0},{2,3},{3,2},{4,5},{5,4},{6,7},{7,6},{8,9},{9,8},{10,11... | collective-permute-start | bytes 786440 | tf_op jit(solution)/shard_map/ppermute | solution.py:25
  12.1 2.6 %collective-permute-start.1 = (bf16[512,256]{1,0:T(8,128)(2,1)S(1)}, bf16[512,256]{1,0:T(8,128)(2,1)S(1)}, u32[]{:S(2)}, u32[]{:S(2)}) collective-permute-start(bf16[512,256]{1,0:T(8,128)(2,1)S(1)} %collective-permute-done.halo), channel_id=1, source_target_pairs={{0,1},{1,0},{2,3},{3,2},{4,5},{5,4},{6,7},{7,6},{8,9},{9,8},{10,11... | collective-permute-start | bytes 786440 | tf_op jit(solution)/shard_map/ppermute | solution.py:25
  12.1 9.5 %collective-permute-start.4 = (bf16[512,256]{1,0:T(8,128)(2,1)S(1)}, bf16[512,256]{1,0:T(8,128)(2,1)S(1)}, u32[]{:S(2)}, u32[]{:S(2)}) collective-permute-start(bf16[512,256]{1,0:T(8,128)(2,1)S(1)} %add_convert_fusion.2), channel_id=1, source_target_pairs={{0,2},{1,3},{2,0},{3,1},{4,6},{5,7},{6,4},{7,5},{8,10},{9,11},{10,... | collective-permute-start | bytes 786440 | tf_op jit(solution)/shard_map/ppermute | solution.py:25
  15.3 6.3 %collective-permute-start.2 = (bf16[512,256]{1,0:T(8,128)(2,1)S(1)}, bf16[512,256]{1,0:T(8,128)(2,1)S(1)}, u32[]{:S(2)}, u32[]{:S(2)}) collective-permute-start(bf16[512,256]{1,0:T(8,128)(2,1)S(1)} %get-tuple-element.18), channel_id=1, source_target_pairs={{0,1},{1,0},{2,3},{3,2},{4,5},{5,4},{6,7},{7,6},{8,9},{9,8},{10,11... | collective-permute-start | bytes 786440 | tf_op jit(solution)/shard_map/ppermute | solution.py:25
  21.7 8.2 %collective-permute-start.6 = (bf16[512,256]{1,0:T(8,128)(2,1)S(1)}, bf16[512,256]{1,0:T(8,128)(2,1)S(1)}, u32[]{:S(2)}, u32[]{:S(2)}) collective-permute-start(bf16[512,256]{1,0:T(8,128)(2,1)S(1)} %add_convert_fusion.1.near0.own), channel_id=1, source_target_pairs={{0,2},{1,3},{2,0},{3,1},{4,6},{5,7},{6,4},{7,5},{8,10},{9,11},{10,... | collective-permute-start | bytes 786440 | tf_op jit(solution)/shard_map/ppermute | solution.py:25
  30.0 9.1 %collective-permute-start.7 = (bf16[512,256]{1,0:T(8,128)(2,1)S(1)}, bf16[512,256]{1,0:T(8,128)(2,1)S(1)}, u32[]{:S(2)}, u32[]{:S(2)}) collective-permute-start(bf16[512,256]{1,0:T(8,128)(2,1)S(1)} %collective-permute-done.6.far), channel_id=1, source_target_pairs={{6,2},{7,3},{0,4},{1,5},{10,6},{11,7},{4,8},{5,9},{14,10},{15,11},... | collective-permute-start | bytes 786440 | tf_op jit(solution)/shard_map/ppermute | solution.py:367
  34.3 4.8 %collective-permute-start.5 = (bf16[512,256]{1,0:T(8,128)(2,1)S(1)}, bf16[512,256]{1,0:T(8,128)(2,1)S(1)}, u32[]{:S(2)}, u32[]{:S(2)}) collective-permute-start(bf16[512,256]{1,0:T(8,128)(2,1)S(1)} %add_convert_fusion.1.near0.own), channel_id=1, source_target_pairs={{0,1},{1,0},{2,3},{3,2},{4,5},{5,4},{6,7},{7,6},{8,9},{9,8},{10,11... | collective-permute-start | bytes 786440 | tf_op jit(solution)/shard_map/ppermute | solution.py:25
  34.4 4.7 %collective-permute-start.10 = (bf16[512,256]{1,0:T(8,128)(2,1)S(1)}, bf16[512,256]{1,0:T(8,128)(2,1)S(1)}, u32[]{:S(2)}, u32[]{:S(2)}) collective-permute-start(bf16[512,256]{1,0:T(8,128)(2,1)S(1)} %collective-permute-done.6.far), channel_id=1, source_target_pairs={{0,1},{1,0},{2,3},{3,2},{4,5},{5,4},{6,7},{7,6},{8,9},{9,8},{10,11... | collective-permute-start | bytes 786440 | tf_op jit(solution)/shard_map/ppermute | solution.py:25
  39.1 1.5 %collective-permute-start.8 = (bf16[512,256]{1,0:T(8,128)(2,1)S(1)}, bf16[512,256]{1,0:T(8,128)(2,1)S(1)}, u32[]{:S(2)}, u32[]{:S(2)}) collective-permute-start(bf16[512,256]{1,0:T(8,128)(2,1)S(1)} %collective-permute-done.7.halo), channel_id=1, source_target_pairs={{0,1},{1,0},{2,3},{3,2},{4,5},{5,4},{6,7},{7,6},{8,9},{9,8},{10,11... | collective-permute-start | bytes 786440 | tf_op jit(solution)/shard_map/ppermute | solution.py:25
  39.7 1.7 %collective-permute-start.11 = (bf16[512,256]{1,0:T(8,128)(2,1)S(1)}, bf16[512,256]{1,0:T(8,128)(2,1)S(1)}, u32[]{:S(2)}, u32[]{:S(2)}) collective-permute-start(bf16[512,256]{1,0:T(8,128)(2,1)S(1)} %get-tuple-element.24), channel_id=1, source_target_pairs={{0,1},{1,0},{2,3},{3,2},{4,5},{5,4},{6,7},{7,6},{8,9},{9,8},{10,11... | collective-permute-start | bytes 786440 | tf_op jit(solution)/shard_map/ppermute | solution.py:25
  41.3 2.3 %collective-permute-start.9 = (bf16[512,256]{1,0:T(8,128)(2,1)S(1)}, bf16[512,256]{1,0:T(8,128)(2,1)S(1)}, u32[]{:S(2)}, u32[]{:S(2)}) collective-permute-start(bf16[512,256]{1,0:T(8,128)(2,1)S(1)} %get-tuple-element.22), channel_id=1, source_target_pairs={{0,1},{1,0},{2,3},{3,2},{4,5},{5,4},{6,7},{7,6},{8,9},{9,8},{10,11... | collective-permute-start | bytes 786440 | tf_op jit(solution)/shard_map/ppermute | solution.py:25
  41.5 8.8 %collective-permute-start.12 = (bf16[512,256]{1,0:T(8,128)(2,1)S(1)}, bf16[512,256]{1,0:T(8,128)(2,1)S(1)}, u32[]{:S(2)}, u32[]{:S(2)}) collective-permute-start(bf16[512,256]{1,0:T(8,128)(2,1)S(1)} %add_convert_fusion), channel_id=1, source_target_pairs={{0,2},{1,3},{2,0},{3,1},{4,6},{5,7},{6,4},{7,5},{8,10},{9,11},{10,... | collective-permute-start | bytes 786440 | tf_op jit(solution)/shard_map/ppermute | solution.py:25
  51.1 1.3 %collective-permute-start.13 = (f32[136,128]{1,0:T(8,128)S(1)}, f32[136,128]{1,0:T(8,128)S(1)}, u32[]{:S(2)}, u32[]{:S(2)}) collective-permute-start(f32[136,128]{1,0:T(8,128)S(1)} %get-tuple-element.26), channel_id=1, source_target_pairs={{0,1},{1,0},{2,3},{3,2},{4,5},{5,4},{6,7},{7,6},{8,9},{9,8},{10,11... | collective-permute-start | bytes 208904 | tf_op jit(solution)/shard_map/ppermute | solution.py:25
  52.4 4.4 %collective-permute-start.14 = (f32[136,128]{1,0:T(8,128)S(1)}, f32[136,128]{1,0:T(8,128)S(1)}, u32[]{:S(2)}, u32[]{:S(2)}) collective-permute-start(f32[136,128]{1,0:T(8,128)S(1)} %add.31), channel_id=1, source_target_pairs={{0,2},{1,9},{2,0},{3,11},{4,6},{5,13},{6,4},{7,15},{8,10},{9,1},{1... | collective-permute-start | bytes 208904 | tf_op jit(solution)/shard_map/ppermute | solution.py:416
  56.8 5.0 %collective-permute-start.15 = (f32[136,128]{1,0:T(8,128)S(1)}, f32[136,128]{1,0:T(8,128)S(1)}, u32[]{:S(2)}, u32[]{:S(2)}) collective-permute-start(f32[136,128]{1,0:T(8,128)S(1)} %add.32), channel_id=1, source_target_pairs={{0,4},{1,17},{2,6},{3,19},{4,0},{5,21},{6,2},{7,23},{8,12},{9,25},... | collective-permute-start | bytes 208904 | tf_op jit(solution)/shard_map/ppermute | solution.py:416
  61.8 4.7 %collective-permute-start.16 = (f32[136,128]{1,0:T(8,128)S(1)}, f32[136,128]{1,0:T(8,128)S(1)}, u32[]{:S(2)}, u32[]{:S(2)}) collective-permute-start(f32[136,128]{1,0:T(8,128)S(1)} %add.33), channel_id=1, source_target_pairs={{0,8},{1,3},{2,10},{3,1},{4,12},{5,7},{6,14},{7,5},{8,0},{9,11},{1... | collective-permute-start | bytes 208904 | tf_op jit(solution)/shard_map/ppermute | solution.py:416
  66.5 5.4 %collective-permute-start.17 = (f32[136,128]{1,0:T(8,128)S(1)}, f32[136,128]{1,0:T(8,128)S(1)}, u32[]{:S(2)}, u32[]{:S(2)}) collective-permute-start(f32[136,128]{1,0:T(8,128)S(1)} %add.34), channel_id=1, source_target_pairs={{0,16},{1,5},{2,18},{3,7},{4,20},{5,1},{6,22},{7,3},{8,24},{9,13},... | collective-permute-start | bytes 208904 | tf_op jit(solution)/shard_map/ppermute | solution.py:416
  71.9 1.3 %collective-permute-start.18 = (f32[136,128]{1,0:T(8,128)S(1)}, f32[136,128]{1,0:T(8,128)S(1)}, u32[]{:S(2)}, u32[]{:S(2)}) collective-permute-start(f32[136,128]{1,0:T(8,128)S(1)} %add.35.mine), channel_id=1, source_target_pairs={{0,1},{1,0},{2,3},{3,2},{4,5},{5,4},{6,7},{7,6},{8,9},{9,8},{10,11... | collective-permute-start | bytes 208904 | tf_op jit(solution)/shard_map/ppermute | solution.py:25
